TPU v7x, 32 devices: a whole 2x2x4 slice. The times are simulated.
32 devices in a mesh: ctx: 8 (over y, x, core), exp: 4 (over z).
Axes of the slice: x: 2, y: 2, z: 4, core: 2. Of those that a mesh axis runs over, the one named last changes fastest.
Arguments:
- lin_query: bfloat16 [1024, 8192], P('ctx', 'exp'), may hold values from -5 to 5
- lin_key: bfloat16 [1024, 8192], P('ctx', 'exp'), may hold values from -5 to 5
- lin_value: bfloat16 [1024, 8192], P('ctx', 'exp'), may hold values from -5 to 5
- log_decay: float32 [1024, 64], P('ctx', 'exp'), may hold values from -1.5 to 0
- lin_gain: float32 [8192], P('exp'), may hold values from 0.25 to 1.75
- moe_input: bfloat16 [192, 6144], P(('ctx', 'exp')), may hold values from -6 to 6
- routes: int32 [192, 2], P(('ctx', 'exp')), may hold values from 0 to 7, all different within a row; in each aligned block of 6 rows (0 to 5, 6 to 11, ...) at most 2 rows name the same one
- route_weight: float32 [192, 2], P(('ctx', 'exp')), may hold values from 0.2 to 1
- gate_weight: bfloat16 [8, 6144, 9216], P('exp', None, 'ctx'), may hold values from -0.078125 to 0.078125
- up_weight: bfloat16 [8, 6144, 9216], P('exp', None, 'ctx'), may hold values from -0.078125 to 0.078125
- down_weight: bfloat16 [8, 9216, 6144], P('exp', 'ctx'), may hold values from -0.0625 to 0.0625
- soft_query: bfloat16 [1024, 8192], P('ctx', 'exp'), may hold values from -5 to 5
- soft_kv: bfloat16 [1024, 8, 2, 128], P('ctx', 'exp'), may hold values from -5 to 5
Outputs:
- lin_out: bfloat16 [1024, 8192], P('ctx', 'exp')
- moe_out: bfloat16 [192, 6144], P(('ctx', 'exp'))
- soft_out: bfloat16 [1024, 8192], P('ctx', 'exp')
Inputs may be any that keep to these rules, and one draw needn't show every extreme that they name: `routes`: within the rows of one device (6 rows) each expert is named by at most 2 of them; the 2 experts of a row differ.
All inputs are finite; a program needn't handle non-finite values.
Results may differ from a plain program's by a relative error of at most 0.009.
Values may be sent and summed in bfloat16 or wider, within the bound.
No kernel may reach another device: no remote copies, remote signals or barrier semaphores. Data moves between devices by JAX's collectives and lax.ppermute only.
A program may use at most 192 MiB of HBM per device.

v0:
```python
import functools
import math

import jax
import jax.numpy as jnp
from jax import lax
from jax.experimental import pallas as pl
from jax.experimental.pallas import tpu as pltpu
from jax.sharding import PartitionSpec as P


TOP = 2
CAP = 2
F32 = jnp.float32
BF16 = jnp.bfloat16
MASKED = -1e30


vmem_spec = pl.BlockSpec(memory_space=pltpu.VMEM)
smem_spec = pl.BlockSpec(memory_space=pltpu.SMEM)
any_spec = pl.BlockSpec(memory_space=pl.ANY)
hbm_spec = pl.BlockSpec(memory_space=pltpu.HBM)


def shape(dims, dtype):
    return jax.ShapeDtypeStruct(tuple(dims), dtype)


def params(mib):
    return pltpu.CompilerParams(vmem_limit_bytes=mib << 20)


def cost(flops, nbytes):
    return pl.CostEstimate(flops=flops, bytes_accessed=nbytes, transcendentals=0)


def swap(value, axis, offset):
    return lax.ppermute(value, axis, [(i, i ^ offset) for i in range(lax.axis_size(axis))])


def tie(*values):
    return lax.optimization_barrier(values)


def in_hbm(*values):
    return [pltpu.with_memory_space_constraint(one, pltpu.HBM) for one in values]


def slot_matrix(flags_ref, routes_ref, rows, slots, here, weight_ref=None):
    named = [[routes_ref[k, r] for k in range(TOP)] for r in range(rows)]
    flat = [one for row in named for one in row]
    at_slot = lax.broadcasted_iota(jnp.int32, (slots, rows), 0)
    at_row = lax.broadcasted_iota(jnp.int32, (slots, rows), 1)
    matrix = jnp.zeros((slots, rows), F32)
    for i, mine in enumerate(flat):
        rank = jnp.int32(0)
        for other in flat[:i]:
            rank = rank + (other == mine).astype(jnp.int32)
        place = (lax.div(mine, here) ^ flags_ref[2]) * here + lax.rem(mine, here)
        slot = place * CAP + rank
        value = 1.0 if weight_ref is None else weight_ref[i % TOP, i // TOP]
        matrix = matrix + jnp.where((at_slot == slot) & (at_row == i // TOP), value, 0.0)
    return matrix


def pack(flags, moe_input, routes, planes, experts):
    rows, width = moe_input.shape
    slots = experts * CAP
    part = width // 2
    each = slots // planes

    def kernel(flags_ref, routes_ref, x_ref, *out_refs):
        matrix = slot_matrix(flags_ref, routes_ref, rows, slots, experts // planes)
        matrix = matrix.astype(BF16)
        for h in range(2):
            at = pl.ds(pl.multiple_of((flags_ref[1] ^ h) * part, 128), part)
            value = jnp.dot(matrix, x_ref[:, at], preferred_element_type=F32)
            for p, out_ref in enumerate(out_refs):
                out_ref[:, h * part : (h + 1) * part] = value[p * each : (p + 1) * each].astype(BF16)

    return pl.pallas_call(
        kernel,
        in_specs=[smem_spec, smem_spec, vmem_spec],
        out_specs=[vmem_spec] * planes,
        out_shape=[shape((each, width), BF16)] * planes,
        compiler_params=params(2),
    )(flags, routes.T, *in_hbm(moe_input))


def arrange(arrived):
    each, width = arrived[0].shape
    part = width // 2

    def kernel(*refs):
        *in_refs, own_ref, other_ref = refs
        for h, out_ref in enumerate((own_ref, other_ref)):
            at = slice(h * part, (h + 1) * part)
            out_ref[...] = jnp.concatenate([one[:, at].astype(F32) for one in in_refs]).astype(BF16)

    return pl.pallas_call(
        kernel,
        in_specs=[vmem_spec] * len(arrived),
        out_specs=[vmem_spec] * 2,
        out_shape=[shape((len(arrived) * each, part), BF16)] * 2,
        compiler_params=params(2),
    )(*arrived)


def unpack(flags, returned, routes, route_weight):
    planes = len(returned)
    each, width = returned[0].shape
    slots = planes * each
    rows = routes.shape[0]
    part = width // 2

    def kernel(flags_ref, routes_ref, weight_ref, *refs):
        *y_refs, out_ref = refs
        matrix = slot_matrix(flags_ref, routes_ref, rows, slots, each // CAP, weight_ref)
        pieces = []
        for _ in range(3):
            pieces.append(matrix.astype(BF16))
            matrix = matrix - pieces[-1].astype(F32)
        for h in range(2):
            y = jnp.concatenate(
                [one[:, h * part : (h + 1) * part].astype(F32) for one in y_refs]
            ).astype(BF16)
            total = None
            for piece in pieces:
                term = lax.dot_general(
                    piece, y, (((0,), (0,)), ((), ())), preferred_element_type=F32
                )
                total = term if total is None else total + term
            at = pl.ds(pl.multiple_of((flags_ref[1] ^ h) * part, 128), part)
            out_ref[:, at] = total.astype(BF16)

    return pl.pallas_call(
        kernel,
        in_specs=[smem_spec] * 3 + [vmem_spec] * planes,
        out_specs=vmem_spec,
        out_shape=shape((rows, width), BF16),
        compiler_params=params(4),
    )(flags, routes.T, route_weight.T, *returned)


def divisor(total, most, unit=128):
    return max(d for d in range(unit, most + 1, unit) if total % d == 0)


def gate_and_up(flags, which, x_half, gate_half, up_weight, sums=None, down_weight=None):
    rows, part = x_half.shape
    experts, _, hidden = gate_half.shape
    deep = divisor(part, 1536)
    chunks = part // deep
    final = sums is not None
    given = 1 if final else 0
    left = max(1, experts - given)
    ahead = columns_ahead(part)
    blocks = lax.axis_size("ctx")
    block = rows // blocks

    def kernel(flags_ref, x_ref, gate_ref, up_ref, *refs):
        if final:
            (gate_in, up_in, up_first, down_ref, inner_ref, early_ref,
             ups, sems, early_sems, x_held) = refs
        else:
            gate_out, up_out, next_ref, ups, sems, next_sem = refs
        half = flags_ref[1] ^ which

        def fetch(e, s):
            at = pl.ds(pl.multiple_of(half * part + s * deep, deep), deep)
            return pltpu.make_async_copy(up_ref.at[e, at], ups.at[e - given, s], sems.at[e - given, s])

        for e in range(given, experts):
            for s in range(chunks):
                fetch(e, s).start()
        if not final:
            rest = pl.ds(pl.multiple_of((1 - half) * part, part), part)
            following = pltpu.make_async_copy(up_ref.at[0, rest], next_ref, next_sem)
            following.start()
        if final:
            early = fetch_ahead(flags_ref[1] ^ 1, part, ahead, down_ref, early_ref, early_sems)
            for copy in early:
                copy.start()
            expert_of = lax.rem(
                lax.div(lax.broadcasted_iota(jnp.int32, (rows, 1), 0), CAP), experts
            )
        if final:
            for k in range(blocks):
                x_held[k * block : (k + 1) * block] = x_ref[(k ^ 1) * block : ((k ^ 1) + 1) * block]
            x_ref = x_held
        for e in range(experts):
            gate = jnp.dot(x_ref[...], gate_ref[e], preferred_element_type=F32)
            if final:
                gate_in[e] = gate_in[e] + gate
            else:
                gate_out[e] = gate
            if e < given:
                weight = up_first[...]
            else:
                for s in range(chunks):
                    fetch(e, s).wait()
                weight = ups[e - given].reshape(part, hidden)
            up = jnp.dot(x_ref[...], weight, preferred_element_type=F32)
            if final:
                gated = gate_in[e]
                value = gated / (1.0 + jnp.exp(-gated)) * (up_in[e] + up)
                here = jnp.broadcast_to(expert_of, (rows, hidden)) == e
                inner_ref[e] = jnp.where(here, value, 0.0).astype(BF16)
            else:
                up_out[e] = up
        if final:
            for copy in early:
                copy.wait()
        else:
            following.wait()

    partial = shape((experts, rows, hidden), F32)
    scratch = [
        pltpu.VMEM((left, chunks, deep, hidden), BF16),
        pltpu.SemaphoreType.DMA((left, chunks)),
    ]
    if final:
        out_shape = [
            pltpu.VMEM((experts, rows, hidden), BF16),
            pltpu.VMEM((experts, hidden, ahead), BF16),
        ]
        scratch = scratch + [
            pltpu.SemaphoreType.DMA((experts,)), pltpu.VMEM((rows, part), BF16)
        ]
        operands, specs = (*sums, *in_hbm(down_weight)), [vmem_spec] * 3 + [hbm_spec]
    else:
        out_shape = [partial, partial, pltpu.VMEM((part, hidden), BF16)]
        scratch = scratch + [pltpu.SemaphoreType.DMA]
        operands, specs = (), []
    return pl.pallas_call(
        kernel,
        in_specs=[smem_spec, vmem_spec, vmem_spec, hbm_spec] + specs,
        out_specs=[vmem_spec] * len(out_shape),
        out_shape=out_shape,
        scratch_shapes=scratch,
        compiler_params=params(18),
        cost_estimate=cost(4 * rows * experts * part * hidden, 4 * experts * part * hidden),
    )(flags, x_half, gate_half, *in_hbm(up_weight), *operands)


def down_step(part):
    return divisor(part, 1024)


def columns_ahead(part):
    wide = down_step(part)
    return max(1, (part // wide) * 2 // 3) * wide


def fetch_ahead(half, part, ahead, weight_ref, to_ref, sems):
    at = pl.ds(pl.multiple_of(half * part, 128), ahead)
    return [
        pltpu.make_async_copy(weight_ref.at[e, :, at], to_ref.at[e], sems.at[e])
        for e in range(to_ref.shape[0])
    ]


def down(flags, which, inner, early, down_weight):
    experts, rows, hidden = inner.shape
    part = down_weight.shape[2] // 2
    wide = down_step(part)
    ahead = early.shape[2]
    done = ahead // wide
    steps = part // wide
    left = max(1, steps - done)
    block = rows // lax.axis_size("ctx")

    def kernel(flags_ref, inner_ref, early_ref, down_ref, out_ref, *refs):
        if which == 1:
            next_ref, downs, sems, next_sems = refs
        else:
            downs, sems = refs
        half = flags_ref[1] ^ which

        def fetch(i):
            at = pl.ds(pl.multiple_of(half * part + i * wide, 128), wide)
            return [
                pltpu.make_async_copy(
                    down_ref.at[e, :, at], downs.at[i - done, e], sems.at[i - done, e]
                )
                for e in range(experts)
            ]

        for i in range(done, steps):
            for copy in fetch(i):
                copy.start()
        if which == 1:
            following = fetch_ahead(flags_ref[1], part, ahead, down_ref, next_ref, next_sems)
            for copy in following:
                copy.start()
        for i in range(steps):
            if i >= done:
                for copy in fetch(i):
                    copy.wait()
            total = None
            for e in range(experts):
                weight = early_ref[e, :, i * wide : (i + 1) * wide] if i < done else downs[i - done, e]
                term = jnp.dot(inner_ref[e], weight, preferred_element_type=F32)
                total = term if total is None else total + term
            at = slice(i * wide, (i + 1) * wide)
            if which == 0:
                out_ref[:, at] = total
            else:
                for k in range(rows // block):
                    out_ref[k * block : (k + 1) * block, at] = total[
                        (k ^ 1) * block : ((k ^ 1) + 1) * block
                    ].astype(BF16)
        if which == 1:
            for copy in following:
                copy.wait()

    scratch = [
        pltpu.VMEM((left, experts, hidden, wide), BF16),
        pltpu.SemaphoreType.DMA((left, experts)),
    ]
    out_shape = [shape((rows, part), BF16 if which == 1 else F32)]
    if which == 1:
        out_shape.append(pltpu.VMEM((experts, hidden, ahead), BF16))
        scratch.append(pltpu.SemaphoreType.DMA((experts,)))
    return pl.pallas_call(
        kernel,
        in_specs=[smem_spec, vmem_spec, vmem_spec, hbm_spec],
        out_specs=[vmem_spec] * len(out_shape),
        out_shape=out_shape,
        scratch_shapes=scratch,
        compiler_params=params(12),
        cost_estimate=cost(rows * experts * 2 * part * hidden, 2 * experts * part * hidden),
    )(flags, inner, early, *in_hbm(down_weight))


def fold_pair(keep, got, pieces):
    rows, part = keep.shape
    each = rows // pieces

    def kernel(keep_ref, got_ref, out_ref, *send_refs):
        out_ref[...] = keep_ref[:each] + got_ref[:each].astype(F32)
        for k, send_ref in enumerate(send_refs, 1):
            at = slice(k * each, (k + 1) * each)
            send_ref[...] = (keep_ref[at] + got_ref[at].astype(F32)).astype(BF16)

    return pl.pallas_call(
        kernel,
        in_specs=[vmem_spec] * 2,
        out_specs=[vmem_spec] * pieces,
        out_shape=[shape((each, part), F32)] + [shape((each, part), BF16)] * (pieces - 1),
        compiler_params=params(4),
    )(keep, got)


def fold_all(keep, got):
    rows, part = keep.shape
    half = rows // 2

    def kernel(keep_ref, *refs):
        *got_refs, out_ref, send_ref = refs
        total = keep_ref[...]
        for one in got_refs:
            total = total + one[...].astype(F32)
        out_ref[...] = total[:half].astype(BF16)
        send_ref[...] = total[half:].astype(BF16)

    return pl.pallas_call(
        kernel,
        in_specs=[vmem_spec] * (1 + len(got)),
        out_specs=[vmem_spec] * 2,
        out_shape=[shape((half, part), BF16)] * 2,
        compiler_params=params(4),
    )(keep, *got)


def finish(own, other, planes):
    rows, part = own.shape
    each = rows // planes

    def kernel(own_ref, other_ref, *out_refs):
        for h, ref in enumerate((own_ref, other_ref)):
            value = ref[...].astype(F32)
            for p, out_ref in enumerate(out_refs):
                out_ref[:, h * part : (h + 1) * part] = value[p * each : (p + 1) * each].astype(BF16)

    return pl.pallas_call(
        kernel,
        in_specs=[vmem_spec] * 2,
        out_specs=[vmem_spec] * planes,
        out_shape=[shape((each, 2 * part), BF16)] * planes,
        compiler_params=params(2),
    )(own, other)


EXTRA = 8


def sums_of(decay_ref):
    length = decay_ref.shape[1]
    row = lax.broadcasted_iota(jnp.int32, (length, length), 0)
    column = lax.broadcasted_iota(jnp.int32, (length, length), 1)
    upper = (row <= column).astype(F32)
    across = jnp.dot(
        decay_ref[...], upper, precision=lax.Precision.HIGHEST, preferred_element_type=F32
    )
    return across.T, across


def put_message(ref, j, state, factor):
    size = state.shape[0]
    ref[j, :size] = state.astype(BF16)
    coarse = factor.astype(BF16)
    fine = (factor - coarse.astype(F32)).astype(BF16)
    which = lax.broadcasted_iota(jnp.int32, (EXTRA, state.shape[1]), 0)
    ref[j, size:] = jnp.where(
        which == 0, coarse.astype(F32), jnp.where(which == 1, fine.astype(F32), 0.0)
    ).astype(BF16)


def get_message(ref, j):
    size = ref.shape[1] - EXTRA
    state = ref[j, :size].astype(F32)
    tail = ref[j, size:].astype(F32)
    return state, tail[0:1] + tail[1:2]


def local_states(flags, lin_key, lin_value, log_decay, gate_weight):
    length, heads = log_decay.shape
    size = lin_key.shape[1] // heads
    half = heads // 2
    experts, width, hidden = gate_weight.shape
    part = width // 2
    chunks = 2

    def kernel(flags_ref, key_ref, value_ref, decay_ref, gate_ref, mine_ref, factor_ref, send_ref,
               own_gate, other_gate, sems):
        step = pl.program_id(0)

        def fetch():
            for h, to in enumerate((own_gate, other_gate)):
                for e in range(experts):
                    for c in range(chunks):
                        rows = part // chunks
                        at = pl.ds(
                            pl.multiple_of((flags_ref[1] ^ h) * part + c * rows, rows), rows
                        )
                        yield pltpu.make_async_copy(
                            gate_ref.at[e, at], to.at[e, c * rows : (c + 1) * rows],
                            sems.at[h, e, c],
                        )

        @pl.when(step == 0)
        def _():
            for copy in fetch():
                copy.start()

        down, _ = sums_of(decay_ref)
        second = (flags_ref[1] ^ step) == 1
        down = jnp.where(second, down[:, half:], down[:, :half])
        last = down[length - 1 : length]
        tail = jnp.exp(last - down)
        factor = jnp.exp(last)
        for j in range(half):
            at = slice(j * size, (j + 1) * size)
            keyed = (key_ref[:, at].astype(F32) * tail[:, j : j + 1]).astype(BF16)
            state = lax.dot_general(
                keyed, value_ref[:, at], (((0,), (0,)), ((), ())), preferred_element_type=F32
            )
            whole = jnp.broadcast_to(factor[:, j : j + 1], (1, size))

            @pl.when(step == 0)
            def _():
                mine_ref[j] = state
                factor_ref[j : j + 1] = whole

            @pl.when(step == 1)
            def _():
                put_message(send_ref, j, state, whole)

        @pl.when(step == 1)
        def _():
            for copy in fetch():
                copy.wait()

    block = pl.BlockSpec((length, half * size), lambda i, p: (0, p[1] ^ i))
    full = lambda dims: pl.BlockSpec(dims, lambda i, p: (0,) * len(dims))
    return pl.pallas_call(
        kernel,
        grid_spec=pltpu.PrefetchScalarGridSpec(
            num_scalar_prefetch=1,
            grid=(2,),
            in_specs=[block, block, full((heads, length)), hbm_spec],
            out_specs=[
                full((half, size, size)),
                full((half, size)),
                full((half, size + EXTRA, size)),
                vmem_spec,
                vmem_spec,
            ],
            scratch_shapes=[pltpu.SemaphoreType.DMA((2, experts, chunks))],
        ),
        out_shape=[
            shape((half, size, size), F32),
            shape((half, size), F32),
            shape((half, size + EXTRA, size), BF16),
            pltpu.VMEM((experts, part, hidden), BF16),
            pltpu.VMEM((experts, part, hidden), BF16),
        ],
        compiler_params=params(8),
        cost_estimate=cost(
            4 * heads * length * size * size,
            4 * length * heads * size + 2 * experts * width * hidden,
        ),
    )(flags, *in_hbm(lin_key, lin_value, log_decay.T, gate_weight))


def join_pair(flags, mine, factor, got):
    half, size, _ = mine.shape

    def kernel(flags_ref, mine_ref, factor_ref, got_ref, sum_ref, sum_factor_ref, send_ref):
        odd = flags_ref[1] == 1
        for j in range(half):
            own, own_factor = mine_ref[j], factor_ref[j : j + 1]
            other, other_factor = get_message(got_ref, j)
            total = jnp.where(odd, own + own_factor * other, other + other_factor * own)
            both = own_factor * other_factor
            sum_ref[j] = total
            sum_factor_ref[j : j + 1] = both
            put_message(send_ref, j, total, both)

    return pl.pallas_call(
        kernel,
        in_specs=[smem_spec] + [vmem_spec] * 3,
        out_specs=[vmem_spec] * 3,
        out_shape=[
            shape((half, size, size), F32),
            shape((half, size), F32),
            shape((half, size + EXTRA, size), BF16),
        ],
        compiler_params=params(8),
    )(flags, mine, factor, got)


def join_group(flags, bit, total, factor, before, before_factor, got):
    half, size, _ = total.shape
    first = before is None
    earlier = () if first else (before, before_factor)

    def kernel(flags_ref, total_ref, factor_ref, got_ref, *refs):
        if first:
            sum_ref, sum_factor_ref, send_ref, before_out, before_factor_out = refs
        else:
            (before_ref, before_factor_ref,
             sum_ref, sum_factor_ref, send_ref, before_out, before_factor_out) = refs
        high = ((flags_ref[0] >> bit) & 1) == 1
        for j in range(half):
            own, own_factor = total_ref[j], factor_ref[j : j + 1]
            other, other_factor = get_message(got_ref, j)
            if first:
                prior, prior_factor = jnp.zeros_like(own), jnp.ones_like(own_factor)
            else:
                prior, prior_factor = before_ref[j], before_factor_ref[j : j + 1]
            before_out[j] = jnp.where(high, prior + prior_factor * other, prior)
            before_factor_out[j : j + 1] = jnp.where(
                high, prior_factor * other_factor, prior_factor
            )
            joined = jnp.where(high, own + own_factor * other, other + other_factor * own)
            both = own_factor * other_factor
            sum_ref[j] = joined
            sum_factor_ref[j : j + 1] = both
            put_message(send_ref, j, joined, both)

    return pl.pallas_call(
        kernel,
        in_specs=[smem_spec] + [vmem_spec] * (3 + len(earlier)),
        out_specs=[vmem_spec] * 5,
        out_shape=[
            shape((half, size, size), F32),
            shape((half, size), F32),
            shape((half, size + EXTRA, size), BF16),
            shape((half, size, size), F32),
            shape((half, size), F32),
        ],
        compiler_params=params(12),
    )(flags, total, factor, got, *earlier)


def join_end(flags, bit, before, before_factor, got, mine, factor, neighbour):
    half, size, _ = mine.shape
    given = [one for one in (before, before_factor, got) if one is not None]

    def kernel(flags_ref, *refs):
        refs = list(refs)
        before_ref = refs.pop(0) if before is not None else None
        before_factor_ref = refs.pop(0) if before is not None else None
        got_ref = refs.pop(0) if got is not None else None
        mine_ref, factor_ref, neighbour_ref, keep_ref, send_ref = refs
        high, odd = ((flags_ref[0] >> bit) & 1) == 1, flags_ref[1] == 1
        for j in range(half):
            state = jnp.zeros((size, size), F32)
            if before_ref is not None:
                state = before_ref[j]
            if got_ref is not None:
                other, _ = get_message(got_ref, j)
                scaled = other if before_ref is None else before_factor_ref[j : j + 1] * other
                state = jnp.where(high, state + scaled, state)
            other, other_factor = get_message(neighbour_ref, j)
            even_state = jnp.where(odd, other, mine_ref[j])
            even_factor = jnp.where(odd, other_factor, factor_ref[j : j + 1])
            for_odd = even_state + even_factor * state
            keep_ref[j] = jnp.where(odd, for_odd, state).astype(BF16)
            send_ref[j] = jnp.where(odd, state, for_odd).astype(BF16)

    return pl.pallas_call(
        kernel,
        in_specs=[smem_spec] + [vmem_spec] * (len(given) + 3),
        out_specs=[vmem_spec] * 2,
        out_shape=[shape((half, size, size), BF16)] * 2,
        compiler_params=params(8),
    )(flags, *given, mine, factor, neighbour)


def lightning(flags, lin_query, lin_key, lin_value, log_decay, lin_gain, near, far):
    length, heads = log_decay.shape
    size = lin_key.shape[1] // heads
    half = heads // 2
    scale = 1.0 / math.sqrt(size)

    def kernel(flags_ref, query_ref, key_ref, value_ref, decay_ref, gain_ref, near_ref, far_ref,
               out_ref):
        down, across = sums_of(decay_ref)
        step = pl.program_id(0)
        second = (flags_ref[1] ^ step) == 1
        down = jnp.where(second, down[:, half:], down[:, :half])
        across = jnp.where(second, across[half:], across[:half])
        risen = jnp.exp(down) * scale
        row = lax.broadcasted_iota(jnp.int32, (length, length), 0)
        column = lax.broadcasted_iota(jnp.int32, (length, length), 1)
        causal = column <= row
        for j in range(half):
            at = slice(j * size, (j + 1) * size)
            query, key, value = query_ref[:, at], key_ref[:, at], value_ref[:, at]
            scores = lax.dot_general(
                query, key, (((1,), (1,)), ((), ())), preferred_element_type=F32
            )
            spread = down[:, j : j + 1] - across[j : j + 1]
            decays = jnp.exp(jnp.where(causal, spread, MASKED))
            mixed = (scores * (decays * scale)).astype(BF16)
            prior = jnp.where(step == 0, near_ref[j], far_ref[j])
            combined = jnp.dot(mixed, value, preferred_element_type=F32)
            combined = combined + risen[:, j : j + 1] * jnp.dot(
                query, prior, preferred_element_type=F32
            )
            square = jnp.mean(combined * combined, axis=-1, keepdims=True) + 1e-06
            out_ref[:, at] = (combined * lax.rsqrt(square) * gain_ref[:, at]).astype(BF16)

    block = pl.BlockSpec((length, half * size), lambda i, p: (0, p[1] ^ i))
    gains = pl.BlockSpec((1, half * size), lambda i, p: (0, p[1] ^ i))
    full = lambda dims: pl.BlockSpec(dims, lambda i, p: (0,) * len(dims))
    return pl.pallas_call(
        kernel,
        grid_spec=pltpu.PrefetchScalarGridSpec(
            num_scalar_prefetch=1,
            grid=(2,),
            in_specs=[
                block, block, block, full((heads, length)), gains,
                full((half, size, size)), full((half, size, size)),
            ],
            out_specs=block,
        ),
        out_shape=shape(lin_query.shape, BF16),
        compiler_params=params(12),
        cost_estimate=cost(6 * heads * length * size * size, 8 * length * heads * size),
    )(flags, lin_query, lin_key, lin_value, log_decay.T, lin_gain.reshape(1, -1), near, far)


def softmax_layer(flags, which, soft_query, pieces, turn, groups, size, heads, so_far=None):
    length, _ = soft_query.shape
    total = sum(one.shape[0] for one in pieces)
    scale = math.log2(math.e) / math.sqrt(size)
    given = () if so_far is None else (so_far,)

    def kernel(flags_ref, query_ref, *refs):
        piece_refs = refs[: len(pieces)]
        out_ref, keys, values, bias = refs[len(pieces) + len(given) :]
        at = 0
        for one in piece_refs:
            count = one.shape[0]
            keys[at : at + count] = one[:, :size]
            values[at : at + count, :size] = one[:, size:]
            at += count
        values[:, size:] = jnp.ones((total, size), BF16)

        @pl.when(pl.program_id(0) == 0)
        def _():
            me = flags_ref[0]
            row = lax.broadcasted_iota(jnp.int32, (length, length), 0)
            column = lax.broadcasted_iota(jnp.int32, (length, length), 1)
            ahead = column - row
            for k in range(total // length):
                source = me ^ (k ^ turn)
                late = ahead + (source - me) * length > 0
                bias[:, k * length : (k + 1) * length] = jnp.where(late, MASKED, 0.0)

        for h in range(heads):
            at = slice(h * size, (h + 1) * size)
            scores = lax.dot_general(
                query_ref[:, at], keys[...], (((1,), (1,)), ((), ())), preferred_element_type=F32
            )
            scores = scores * scale + bias[...]
            weights = jnp.exp2(scores - jnp.max(scores, axis=-1, keepdims=True))
            mixed = jnp.dot(weights.astype(BF16), values[...], preferred_element_type=F32)
            out_ref[:, at] = (mixed[:, :size] / mixed[:, size:]).astype(BF16)

    place = lambda g, f: (0, g if which is None else (f[1] ^ which) * groups + g)
    block = pl.BlockSpec((length, heads * size), place)
    return pl.pallas_call(
        kernel,
        grid_spec=pltpu.PrefetchScalarGridSpec(
            num_scalar_prefetch=1,
            grid=(groups,),
            in_specs=[block]
            + [pl.BlockSpec((one.shape[0], 2 * size), lambda g, f: (0, g)) for one in pieces]
            + [any_spec] * len(given),
            out_specs=block,
            scratch_shapes=[
                pltpu.VMEM((total, size), BF16),
                pltpu.VMEM((total, 2 * size), BF16),
                pltpu.VMEM((length, total), F32),
            ],
        ),
        out_shape=shape(soft_query.shape, BF16),
        input_output_aliases={2 + len(pieces): 0} if given else {},
        compiler_params=params(12),
        cost_estimate=cost(
            4 * groups * heads * size * length * total, 4 * length * groups * heads * size
        ),
    )(flags, soft_query, *pieces, *given)


def on_device(
    lin_query, lin_key, lin_value, log_decay, lin_gain,
    moe_input, routes, route_weight, gate_weight, up_weight, down_weight,
    soft_query, soft_kv,
):
    count, planes = lax.axis_size("ctx"), lax.axis_size("exp")
    me = lax.axis_index("ctx").astype(jnp.int32)
    flags = jnp.stack([me, me & 1, lax.axis_index("exp").astype(jnp.int32)])
    high = list(range(1, count.bit_length() - 1))
    chips = range(2, count, 2)
    experts = gate_weight.shape[0] * planes
    groups, size = soft_kv.shape[1], soft_kv.shape[3]
    heads = soft_query.shape[1] // size // groups
    split = groups % 2 == 0
    kv_width = groups * 2 * size
    after = lambda value: tie(flags, value)[0]

    held = soft_kv.reshape(soft_kv.shape[0], kv_width)
    kv_other = held
    if split:
        odd = flags[1] == 1
        first, second = held[:, : kv_width // 2], held[:, kv_width // 2 :]
        held, kv_other = jnp.where(odd, second, first), jnp.where(odd, first, second)

    outgoing = pack(tie(flags, held)[0], moe_input, routes, planes, experts)
    arrived = [outgoing[0]] + [swap(outgoing[p], "exp", p) for p in range(1, planes)]
    kv_other = tie(kv_other, outgoing[0])[0]
    held = jnp.concatenate([held, swap(kv_other, "ctx", 1)])
    kv_got = [swap(held, "ctx", j) for j in chips]
    *arrived, held = tie(*arrived, held)

    own, other = arrange(arrived)
    rows = jnp.concatenate([own, swap(other, "ctx", 1)])
    got = [swap(rows, "ctx", j) for j in chips]
    mine, factor, message, own_gate, other_gate = local_states(
        after(rows), lin_key, lin_value, log_decay, gate_weight
    )
    *got, message = tie(*got, message)
    near = jnp.concatenate([rows, *got])
    far = swap(near, "ctx", 1)
    neighbour = swap(message, "ctx", 1)

    sums = gate_and_up(flags, 0, near, own_gate, up_weight)
    total, total_factor, message = join_pair(after(sums[0]), mine, factor, neighbour)
    far, message = tie(far, message)
    before = before_factor = got = None
    if high:
        got = swap(message, "ctx", 2)
    inner, early = gate_and_up(
        flags, 1, far, other_gate, up_weight, sums, down_weight
    )
    for i, b in enumerate(high[:-1]):
        total, total_factor, message, before, before_factor = join_group(
            after(inner), b, total, total_factor, before, before_factor, got
        )
        got = swap(message, "ctx", 1 << high[i + 1])
    inner, message = tie(inner, message)
    send, early = down(flags, 1, inner, early, down_weight)
    summed = swap(send, "ctx", 1)
    keep, = down(after(send), 0, inner, early, down_weight)

    keep, *sends = fold_pair(keep, summed, count // 2)
    got_sums = [swap(one, "ctx", j) for j, one in zip(chips, sends)]
    attention = functools.partial(softmax_layer, size=size, heads=heads)
    pieces = [held, *kv_got]
    if split:
        whole = jnp.concatenate(tie(keep, *pieces)[1:])
        kv_far = swap(whole, "ctx", 1)
        soft_out = attention(after(sends[0]), 0, soft_query, [whole], 0, groups // 2)
        soft_out = attention(
            after(soft_out), 1, soft_query, [kv_far], 1, groups // 2, so_far=soft_out
        )
    else:
        soft_out = attention(after(sends[0]), None, soft_query, pieces, 0, groups)
    *got_sums, soft_out = tie(*got_sums, soft_out)
    own, send = fold_all(keep, got_sums)
    other = swap(send, "ctx", 1)
    last = high[-1] if high else 0
    state_near, state_send = join_end(
        after(send), last, before, before_factor, got, mine, factor, neighbour
    )
    state_far = swap(state_send, "ctx", 1)
    result = finish(own, other, planes)
    returned = [result[0]] + [swap(result[p], "exp", p) for p in range(1, planes)]
    lin_out = lightning(
        after(result[0]), lin_query, lin_key, lin_value, log_decay, lin_gain,
        state_near, state_far,
    )
    *returned, lin_out = tie(*returned, lin_out)
    moe_out = unpack(flags, returned, routes, route_weight)
    return (lin_out, moe_out, soft_out)


def solution(mesh):
    placed = (
        P("ctx", "exp"),
        P("ctx", "exp"),
        P("ctx", "exp"),
        P("ctx", "exp"),
        P("exp"),
        P(("ctx", "exp"), None),
        P(("ctx", "exp"), None),
        P(("ctx", "exp"), None),
        P("exp", None, "ctx"),
        P("exp", None, "ctx"),
        P("exp", "ctx", None),
        P("ctx", "exp"),
        P("ctx", "exp", None, None),
    )

    return jax.shard_map(
        on_device,
        mesh=mesh,
        in_specs=placed,
        out_specs=(P("ctx", "exp"), P(("ctx", "exp"), None), P("ctx", "exp")),
        check_vma=False,
    )
```

profile of v0, /device:TPU:0, one launch (start us, length us, event | category | flops | bytes accessed | tf_op | source)
XLA Modules:
  0.0 100.2 jit_solution(14793929125359490964)
XLA Ops:
  0.6 1.0 reshape.12
  1.7 0.7 copy-done.6
  2.4 1.2 %shard_map.148 = (bf16[4,6144]{1,0:T(4,128)(2,1)S(1)}, bf16[4,6144]{1,0:T(4,128)(2,1)S(1)}, bf16[4,6144]{1,0:T(4,128)(2,1)S(1)}, bf16[4,6144]{1,0:T(4,128)(2,1)S(1)}) custom-call(s32[3]{0:T(128)S(1)} %pad_add_fusion.flags_ref, s32[2,6]{1,0:T(2,128)S(1)} %bitcast.10, bf16[6,6144]{1,0:T(8,128)(2,1)} %x_ref.1), custom_call_target="tpu_custom_call" | custom-call | tf_op jit(solution)/shard_map/pallas_call | solution.py:81
  4.1 2.6 %collective-permute-start = (bf16[4,6144]{1,0:T(4,128)(2,1)S(1)}, bf16[4,6144]{1,0:T(4,128)(2,1)S(1)}, u32[]{:S(2)}, u32[]{:S(2)}) collective-permute-start(bf16[4,6144]{1,0:T(4,128)(2,1)S(1)} %get-tuple-element.76), channel_id=1, source_target_pairs={{0,1},{1,0},{2,3},{3,2},{4,5},{5,4},{6,7},{7,6},{8,9},{9,8},{10,11... | collective-permute-start | bytes 147464 | tf_op jit(solution)/shard_map/ppermute | solution.py:38
  6.8 2.6 %collective-permute-start.1 = (bf16[4,6144]{1,0:T(4,128)(2,1)S(1)}, bf16[4,6144]{1,0:T(4,128)(2,1)S(1)}, u32[]{:S(2)}, u32[]{:S(2)}) collective-permute-start(bf16[4,6144]{1,0:T(4,128)(2,1)S(1)} %get-tuple-element.77), channel_id=1, source_target_pairs={{0,2},{1,3},{2,0},{3,1},{4,6},{5,7},{6,4},{7,5},{8,10},{9,11},{10,... | collective-permute-start | bytes 147464 | tf_op jit(solution)/shard_map/ppermute | solution.py:38
  9.4 3.5 %collective-permute-done.1.refs_2_ = bf16[4,6144]{1,0:T(4,128)(2,1)S(1)} collective-permute-done((bf16[4,6144]{1,0:T(4,128)(2,1)S(1)}, bf16[4,6144]{1,0:T(4,128)(2,1)S(1)}, u32[]{:S(2)}, u32[]{:S(2)}) %collective-permute-start.1) | collective-permute-done | bytes 49184 | tf_op jit(solution)/shard_map/ppermute | solution.py:38
  12.9 2.4 %collective-permute-done.2.refs_3_ = bf16[4,6144]{1,0:T(4,128)(2,1)S(1)} collective-permute-done((bf16[4,6144]{1,0:T(4,128)(2,1)S(1)}, bf16[4,6144]{1,0:T(4,128)(2,1)S(1)}, u32[]{:S(2)}, u32[]{:S(2)}) %collective-permute-start.2) | collective-permute-done | bytes 49184 | tf_op jit(solution)/shard_map/ppermute | solution.py:38
  15.4 1.3 %collective-permute-done.4 = bf16[16,3072]{1,0:T(8,128)(2,1)S(1)} collective-permute-done((bf16[16,3072]{1,0:T(8,128)(2,1)S(1)}, bf16[16,3072]{1,0:T(8,128)(2,1)S(1)}, u32[]{:S(2)}, u32[]{:S(2)}) %collective-permute-start.4) | collective-permute-done | bytes 98336 | tf_op jit(solution)/shard_map/ppermute | solution.py:38
  16.7 1.6 %collective-permute-start.5 = (bf16[32,3072]{1,0:T(8,128)(2,1)S(1)}, bf16[32,3072]{1,0:T(8,128)(2,1)S(1)}, u32[]{:S(2)}, u32[]{:S(2)}) collective-permute-start(bf16[32,3072]{1,0:T(8,128)(2,1)S(1)} %get-tuple-element.147), channel_id=1, source_target_pairs={{0,8},{4,12},{8,0},{12,4},{16,24},{20,28},{24,16},{28,20},{1,9},{5... | collective-permute-start | bytes 589832 | tf_op jit(solution)/shard_map/ppermute | solution.py:38
  18.3 1.5 %collective-permute-start.6 = (bf16[32,3072]{1,0:T(8,128)(2,1)S(1)}, bf16[32,3072]{1,0:T(8,128)(2,1)S(1)}, u32[]{:S(2)}, u32[]{:S(2)}) collective-permute-start(bf16[32,3072]{1,0:T(8,128)(2,1)S(1)} %get-tuple-element.147), channel_id=1, source_target_pairs={{0,16},{4,20},{8,24},{12,28},{16,0},{20,4},{24,8},{28,12},{1,17},{... | collective-permute-start | bytes 589832 | tf_op jit(solution)/shard_map/ppermute | solution.py:38
  20.3 11.1 %shard_map.150 = (f32[8,128,128]{2,1,0:T(8,128)S(1)}, f32[8,128]{1,0:T(8,128)S(1)}, bf16[8,136,128]{2,1,0:T(8,128)(2,1)S(1)}, bf16[2,3072,1152]{2,1,0:T(8,128)(2,1)S(1)}, bf16[2,3072,1152]{2,1,0:T(8,128)(2,1)S(1)}) custom-call(s32[3]{0:T(128)S(1)} %pad_add_fusion.flags_ref, bf16[128,2048]{1,0:T(8,128)(2,1)} %key_ref.3, bf16[128,2048]{1,0:T(8,128)(2,1)} %value_ref.3, ...), custom_call_target="tpu_custom_call" | custom-call | flops 134217728 | bytes 29360128 | tf_op jit(solution)/shard_map/pallas_call | solution.py:487
  32.0 7.7 %shard_map.151 = (f32[2,128,1152]{2,1,0:T(8,128)S(1)}, f32[2,128,1152]{2,1,0:T(8,128)S(1)}, bf16[3072,1152]{1,0:T(8,128)(2,1)S(1)}) custom-call(s32[3]{0:T(128)S(1)} %pad_add_fusion.flags_ref, bf16[128,3072]{1,0:T(8,128)(2,1)S(1)} %constant_dynamic-update-slice_fusion.2.x_ref, bf16[2,3072,1152]{2,1,0:T(8,128)(2,1)S(1)} %get-tuple-element.91.gate_ref, ...), custom_call_target="tpu_custom_call" | custom-call | flops 3623878656 | bytes 28311552 | tf_op jit(solution)/shard_map/pallas_call | solution.py:235
  40.5 1.6 %collective-permute-start.10 = (bf16[8,136,128]{2,1,0:T(8,128)(2,1)S(1)}, bf16[8,136,128]{2,1,0:T(8,128)(2,1)S(1)}, u32[]{:S(2)}, u32[]{:S(2)}) collective-permute-start(bf16[8,136,128]{2,1,0:T(8,128)(2,1)S(1)} %get-tuple-element.106), channel_id=1, source_target_pairs={{0,8},{4,12},{8,0},{12,4},{16,24},{20,28},{24,16},{28,20},{1,9},{5... | collective-permute-start | bytes 835592 | tf_op jit(solution)/shard_map/ppermute | solution.py:38
  42.0 10.9 %shard_map.153 = (bf16[2,128,1152]{2,1,0:T(8,128)(2,1)S(1)}, bf16[2,1152,2048]{2,1,0:T(8,128)(2,1)S(1)}) custom-call(s32[3]{0:T(128)S(1)} %pad_add_fusion.flags_ref, bf16[128,3072]{1,0:T(8,128)(2,1)S(1)} %collective-permute-done.8.x_ref, bf16[2,3072,1152]{2,1,0:T(8,128)(2,1)S(1)} %get-tuple-element.99.gate_ref, bf16[2,6144,1152]{2,1,0:T(8,128)(2,1)} %up_ref.3, ...), custom_call_target="tpu_custom_call" | custom-call | flops 3623878656 | bytes 28311552 | tf_op jit(solution)/shard_map/pallas_call | solution.py:235
  52.9 1.5 %shard_map.154 = (f32[8,128,128]{2,1,0:T(8,128)}, f32[8,128]{1,0:T(8,128)}, bf16[8,136,128]{2,1,0:T(8,128)(2,1)S(1)}, f32[8,128,128]{2,1,0:T(8,128)S(1)}, f32[8,128]{1,0:T(8,128)S(1)}) custom-call(s32[3]{0:T(128)S(1)} %pad_add_fusion.flags_ref, f32[8,128,128]{2,1,0:T(8,128)S(1)} %get-tuple-element.104.total_ref, f32[8,128]{1,0:T(8,128)S(1)} %get-tuple-element.105.factor_ref, ...), custom_call_target="tpu_custom_call" | custom-call | tf_op jit(solution)/shard_map/pallas_call | solution.py:573
  54.4 5.9 %shard_map.155 = (bf16[128,3072]{1,0:T(8,128)(2,1)S(1)}, bf16[2,1152,2048]{2,1,0:T(8,128)(2,1)S(1)}) custom-call(s32[3]{0:T(128)S(1)} %pad_add_fusion.flags_ref, bf16[2,128,1152]{2,1,0:T(8,128)(2,1)S(1)} %get-tuple-element.108.inner_ref, bf16[2,1152,2048]{2,1,0:T(8,128)(2,1)S(1)} %get-tuple-element.109.early_ref, bf16[2,1152,6144]{2,1,0:T(8,128)(2,1)} %down_ref.3), custom_call_target="tpu_custom_call" | custom-call | flops 1811939328 | bytes 14155776 | tf_op jit(solution)/shard_map/pallas_call | solution.py:325
  61.0 1.5 %collective-permute-start.16 = (bf16[256,256]{1,0:T(8,128)(2,1)S(1)}, bf16[256,256]{1,0:T(8,128)(2,1)S(1)}, u32[]{:S(2)}, u32[]{:S(2)}) collective-permute-start(bf16[256,256]{1,0:T(8,128)(2,1)S(1)} %pad_maximum_fusion), channel_id=1, source_target_pairs={{0,16},{4,20},{8,24},{12,28},{16,0},{20,4},{24,8},{28,12},{1,17},{... | collective-permute-start | bytes 393224 | tf_op jit(solution)/shard_map/ppermute | solution.py:38
  62.5 1.4 %collective-permute-start.17 = (bf16[256,256]{1,0:T(8,128)(2,1)S(1)}, bf16[256,256]{1,0:T(8,128)(2,1)S(1)}, u32[]{:S(2)}, u32[]{:S(2)}) collective-permute-start(bf16[256,256]{1,0:T(8,128)(2,1)S(1)} %pad_maximum_fusion), channel_id=1, source_target_pairs={{0,24},{4,28},{8,16},{12,20},{16,8},{20,12},{24,0},{28,4},{1,25},{... | collective-permute-start | bytes 393224 | tf_op jit(solution)/shard_map/ppermute | solution.py:38
  64.0 3.8 %shard_map.156.keep_ref = f32[128,3072]{1,0:T(8,128)S(1)} custom-call(s32[3]{0:T(128)S(1)} %pad_add_fusion.flags_ref, bf16[2,128,1152]{2,1,0:T(8,128)(2,1)S(1)} %get-tuple-element.108.inner_ref, bf16[2,1152,2048]{2,1,0:T(8,128)(2,1)S(1)} %get-tuple-element.112.early_ref, bf16[2,1152,6144]{2,1,0:T(8,128)(2,1)} %down_ref.3), custom_call_target="tpu_custom_call" | custom-call | flops 1811939328 | bytes 14155776 | tf_op jit(solution)/shard_map/pallas_call | solution.py:325
  68.5 1.6 %collective-permute-done.17 = bf16[256,256]{1,0:T(8,128)(2,1)S(1)} collective-permute-done((bf16[256,256]{1,0:T(8,128)(2,1)S(1)}, bf16[256,256]{1,0:T(8,128)(2,1)S(1)}, u32[]{:S(2)}, u32[]{:S(2)}) %collective-permute-start.17) | collective-permute-done | bytes 131104 | tf_op jit(solution)/shard_map/ppermute | solution.py:38
  70.2 0.9 collective-permute-start.23
  71.1 1.5 %collective-permute-start.12 = (bf16[32,3072]{1,0:T(8,128)(2,1)S(1)}, bf16[32,3072]{1,0:T(8,128)(2,1)S(1)}, u32[]{:S(2)}, u32[]{:S(2)}) collective-permute-start(bf16[32,3072]{1,0:T(8,128)(2,1)S(1)} %get-tuple-element.114), channel_id=1, source_target_pairs={{0,8},{4,12},{8,0},{12,4},{16,24},{20,28},{24,16},{28,20},{1,9},{5... | collective-permute-start | bytes 589832 | tf_op jit(solution)/shard_map/ppermute | solution.py:38
  73.1 1.5 %collective-permute-start.14 = (bf16[32,3072]{1,0:T(8,128)(2,1)S(1)}, bf16[32,3072]{1,0:T(8,128)(2,1)S(1)}, u32[]{:S(2)}, u32[]{:S(2)}) collective-permute-start(bf16[32,3072]{1,0:T(8,128)(2,1)S(1)} %get-tuple-element.116), channel_id=1, source_target_pairs={{0,24},{4,28},{8,16},{12,20},{16,8},{20,12},{24,0},{28,4},{1,25},{... | collective-permute-start | bytes 589832 | tf_op jit(solution)/shard_map/ppermute | solution.py:38
  74.6 3.1 %shard_map.158.refs_1_ = bf16[128,2048]{1,0:T(8,128)(2,1)} custom-call(s32[3]{0:T(128)S(1)} %pad_add_fusion.flags_ref, bf16[128,2048]{1,0:T(8,128)(2,1)S(1)} %copy-done.2, bf16[1024,256]{1,0:T(8,128)(2,1)S(1)} %constant_dynamic-update-slice_fusion.7.refs_0_), custom_call_target="tpu_custom_call" | custom-call | flops 536870912 | bytes 524288 | tf_op jit(solution)/shard_map/pallas_call | solution.py:717
  77.7 3.1 %shard_map.159 = bf16[128,2048]{1,0:T(8,128)(2,1)} custom-call(s32[3]{0:T(128)S(1)} %pad_add_fusion.flags_ref, bf16[128,2048]{1,0:T(8,128)(2,1)S(1)} %copy-done.2, bf16[1024,256]{1,0:T(8,128)(2,1)S(1)} %collective-permute-done.18.refs_0_, bf16[128,2048]{1,0:T(8,128)(2,1)} %shard_map.158.refs_1_), custom_call_target="tpu_custom_call", output_to_operand_aliasing={{}: (3, {})} | custom-call | flops 536870912 | bytes 524288 | tf_op jit(solution)/shard_map/pallas_call | solution.py:717
  80.8 6.9 %collective-permute-done.13.refs_1_ = bf16[32,3072]{1,0:T(8,128)(2,1)S(1)} collective-permute-done((bf16[32,3072]{1,0:T(8,128)(2,1)S(1)}, bf16[32,3072]{1,0:T(8,128)(2,1)S(1)}, u32[]{:S(2)}, u32[]{:S(2)}) %collective-permute-start.13) | collective-permute-done | bytes 196640 | tf_op jit(solution)/shard_map/ppermute | solution.py:38
  87.8 0.7 shard_map.162
  89.2 1.2 %collective-permute-done.19.other_ref = bf16[16,3072]{1,0:T(8,128)(2,1)S(1)} collective-permute-done((bf16[16,3072]{1,0:T(8,128)(2,1)S(1)}, bf16[16,3072]{1,0:T(8,128)(2,1)S(1)}, u32[]{:S(2)}, u32[]{:S(2)}) %collective-permute-start.19) | collective-permute-done | bytes 98336 | tf_op jit(solution)/shard_map/ppermute | solution.py:38
  90.4 1.9 %collective-permute-start.21 = (bf16[4,6144]{1,0:T(4,128)(2,1)S(1)}, bf16[4,6144]{1,0:T(4,128)(2,1)S(1)}, u32[]{:S(2)}, u32[]{:S(2)}) collective-permute-start(bf16[4,6144]{1,0:T(4,128)(2,1)S(1)} %get-tuple-element.131), channel_id=1, source_target_pairs={{0,2},{1,3},{2,0},{3,1},{4,6},{5,7},{6,4},{7,5},{8,10},{9,11},{10,... | collective-permute-start | bytes 147464 | tf_op jit(solution)/shard_map/ppermute | solution.py:38
  92.3 2.5 %collective-permute-start.22 = (bf16[4,6144]{1,0:T(4,128)(2,1)S(1)}, bf16[4,6144]{1,0:T(4,128)(2,1)S(1)}, u32[]{:S(2)}, u32[]{:S(2)}) collective-permute-start(bf16[4,6144]{1,0:T(4,128)(2,1)S(1)} %get-tuple-element.132), channel_id=1, source_target_pairs={{0,3},{1,2},{2,1},{3,0},{4,7},{5,6},{6,5},{7,4},{8,11},{9,10},{10,... | collective-permute-start | bytes 147464 | tf_op jit(solution)/shard_map/ppermute | solution.py:38
  94.8 3.6 %shard_map.163 = bf16[128,2048]{1,0:T(8,128)(2,1)} custom-call(s32[3]{0:T(128)S(1)} %pad_add_fusion.flags_ref, bf16[128,2048]{1,0:T(8,128)(2,1)S(1)} %copy-done.3, bf16[128,2048]{1,0:T(8,128)(2,1)S(1)} %copy-done, bf16[128,2048]{1,0:T(8,128)(2,1)S(1)} %copy-done.1, f32[16,128]{1,0:T(8,128)S(1)} %bitcast.8, f32[1,2048]{1,0:T(1,128)S(1)} %bitcast.9, ...), custom_call_target="tpu_custom_call" | custom-call | flops 201326592 | bytes 2097152 | tf_op jit(solution)/shard_map/pallas_call | solution.py:660
  98.5 1.7 %shard_map.164 = bf16[6,6144]{1,0:T(8,128)(2,1)} custom-call(s32[3]{0:T(128)S(1)} %pad_add_fusion.flags_ref, s32[2,6]{1,0:T(2,128)S(1)} %bitcast.11, f32[2,6]{1,0:T(2,128)S(1)} %bitcast.12, bf16[4,6144]{1,0:T(4,128)(2,1)S(1)} %get-tuple-element.140.refs_0_, bf16[4,6144]{1,0:T(4,128)(2,1)S(1)} %collective-permute-done.20.refs_1_, ...), custom_call_target="tpu_custom_call" | custom-call | tf_op jit(solution)/shard_map/pallas_call | solution.py:136
  (66 shorter events, 5.2 us)
Async XLA Ops:
  3.6 5.8 %collective-permute-start.3 = (bf16[128,256]{1,0:T(8,128)(2,1)S(1)}, bf16[128,256]{1,0:T(8,128)(2,1)S(1)}, u32[]{:S(2)}, u32[]{:S(2)}) collective-permute-start(bf16[128,256]{1,0:T(8,128)(2,1)S(1)} %get-tuple-element.79), channel_id=1, source_target_pairs={{0,4},{4,0},{8,12},{12,8},{16,20},{20,16},{24,28},{28,24},{1,5},{5... | collective-permute-start | bytes 196616 | tf_op jit(solution)/shard_map/ppermute | solution.py:38
  4.1 5.3 %collective-permute-start = (bf16[4,6144]{1,0:T(4,128)(2,1)S(1)}, bf16[4,6144]{1,0:T(4,128)(2,1)S(1)}, u32[]{:S(2)}, u32[]{:S(2)}) collective-permute-start(bf16[4,6144]{1,0:T(4,128)(2,1)S(1)} %get-tuple-element.76), channel_id=1, source_target_pairs={{0,1},{1,0},{2,3},{3,2},{4,5},{5,4},{6,7},{7,6},{8,9},{9,8},{10,11... | collective-permute-start | bytes 147464 | tf_op jit(solution)/shard_map/ppermute | solution.py:38
  6.8 6.1 %collective-permute-start.1 = (bf16[4,6144]{1,0:T(4,128)(2,1)S(1)}, bf16[4,6144]{1,0:T(4,128)(2,1)S(1)}, u32[]{:S(2)}, u32[]{:S(2)}) collective-permute-start(bf16[4,6144]{1,0:T(4,128)(2,1)S(1)} %get-tuple-element.77), channel_id=1, source_target_pairs={{0,2},{1,3},{2,0},{3,1},{4,6},{5,7},{6,4},{7,5},{8,10},{9,11},{10,... | collective-permute-start | bytes 147464 | tf_op jit(solution)/shard_map/ppermute | solution.py:38
  9.4 5.9 %collective-permute-start.2 = (bf16[4,6144]{1,0:T(4,128)(2,1)S(1)}, bf16[4,6144]{1,0:T(4,128)(2,1)S(1)}, u32[]{:S(2)}, u32[]{:S(2)}) collective-permute-start(bf16[4,6144]{1,0:T(4,128)(2,1)S(1)} %get-tuple-element.78), channel_id=1, source_target_pairs={{0,3},{1,2},{2,1},{3,0},{4,7},{5,6},{6,5},{7,4},{8,11},{9,10},{10,... | collective-permute-start | bytes 147464 | tf_op jit(solution)/shard_map/ppermute | solution.py:38
  15.3 1.4 %collective-permute-start.4 = (bf16[16,3072]{1,0:T(8,128)(2,1)S(1)}, bf16[16,3072]{1,0:T(8,128)(2,1)S(1)}, u32[]{:S(2)}, u32[]{:S(2)}) collective-permute-start(bf16[16,3072]{1,0:T(8,128)(2,1)S(1)} %get-tuple-element.85), channel_id=1, source_target_pairs={{0,4},{4,0},{8,12},{12,8},{16,20},{20,16},{24,28},{28,24},{1,5},{5... | collective-permute-start | bytes 294920 | tf_op jit(solution)/shard_map/ppermute | solution.py:38
  16.7 14.7 %collective-permute-start.5 = (bf16[32,3072]{1,0:T(8,128)(2,1)S(1)}, bf16[32,3072]{1,0:T(8,128)(2,1)S(1)}, u32[]{:S(2)}, u32[]{:S(2)}) collective-permute-start(bf16[32,3072]{1,0:T(8,128)(2,1)S(1)} %get-tuple-element.147), channel_id=1, source_target_pairs={{0,8},{4,12},{8,0},{12,4},{16,24},{20,28},{24,16},{28,20},{1,9},{5... | collective-permute-start | bytes 589832 | tf_op jit(solution)/shard_map/ppermute | solution.py:38
  18.3 13.1 %collective-permute-start.6 = (bf16[32,3072]{1,0:T(8,128)(2,1)S(1)}, bf16[32,3072]{1,0:T(8,128)(2,1)S(1)}, u32[]{:S(2)}, u32[]{:S(2)}) collective-permute-start(bf16[32,3072]{1,0:T(8,128)(2,1)S(1)} %get-tuple-element.147), channel_id=1, source_target_pairs={{0,16},{4,20},{8,24},{12,28},{16,0},{20,4},{24,8},{28,12},{1,17},{... | collective-permute-start | bytes 589832 | tf_op jit(solution)/shard_map/ppermute | solution.py:38
  19.8 11.6 %collective-permute-start.7 = (bf16[32,3072]{1,0:T(8,128)(2,1)S(1)}, bf16[32,3072]{1,0:T(8,128)(2,1)S(1)}, u32[]{:S(2)}, u32[]{:S(2)}) collective-permute-start(bf16[32,3072]{1,0:T(8,128)(2,1)S(1)} %get-tuple-element.147), channel_id=1, source_target_pairs={{0,24},{4,28},{8,16},{12,20},{16,8},{20,12},{24,0},{28,4},{1,25},{... | collective-permute-start | bytes 589832 | tf_op jit(solution)/shard_map/ppermute | solution.py:38
  31.5 9.0 %collective-permute-start.8 = (bf16[128,3072]{1,0:T(8,128)(2,1)S(1)}, bf16[128,3072]{1,0:T(8,128)(2,1)S(1)}, u32[]{:S(2)}, u32[]{:S(2)}) collective-permute-start(bf16[128,3072]{1,0:T(8,128)(2,1)S(1)} %constant_dynamic-update-slice_fusion.2.x_ref), channel_id=1, source_target_pairs={{0,4},{4,0},{8,12},{12,8},{16,20},{20,16},{24,28},{28,24},{1,5},{5... | collective-permute-start | bytes 2359304 | tf_op jit(solution)/shard_map/ppermute | solution.py:38
  31.5 8.2 %collective-permute-start.9 = (bf16[8,136,128]{2,1,0:T(8,128)(2,1)S(1)}, bf16[8,136,128]{2,1,0:T(8,128)(2,1)S(1)}, u32[]{:S(2)}, u32[]{:S(2)}) collective-permute-start(bf16[8,136,128]{2,1,0:T(8,128)(2,1)S(1)} %get-tuple-element.96), channel_id=1, source_target_pairs={{0,4},{4,0},{8,12},{12,8},{16,20},{20,16},{24,28},{28,24},{1,5},{5... | collective-permute-start | bytes 835592 | tf_op jit(solution)/shard_map/ppermute | solution.py:38
  40.5 12.5 %collective-permute-start.10 = (bf16[8,136,128]{2,1,0:T(8,128)(2,1)S(1)}, bf16[8,136,128]{2,1,0:T(8,128)(2,1)S(1)}, u32[]{:S(2)}, u32[]{:S(2)}) collective-permute-start(bf16[8,136,128]{2,1,0:T(8,128)(2,1)S(1)} %get-tuple-element.106), channel_id=1, source_target_pairs={{0,8},{4,12},{8,0},{12,4},{16,24},{20,28},{24,16},{28,20},{1,9},{5... | collective-permute-start | bytes 835592 | tf_op jit(solution)/shard_map/ppermute | solution.py:38
  60.3 7.6 %collective-permute-start.11 = (bf16[128,3072]{1,0:T(8,128)(2,1)S(1)}, bf16[128,3072]{1,0:T(8,128)(2,1)S(1)}, u32[]{:S(2)}, u32[]{:S(2)}) collective-permute-start(bf16[128,3072]{1,0:T(8,128)(2,1)S(1)} %get-tuple-element.110), channel_id=1, source_target_pairs={{0,4},{4,0},{8,12},{12,8},{16,20},{20,16},{24,28},{28,24},{1,5},{5... | collective-permute-start | bytes 2359304 | tf_op jit(solution)/shard_map/ppermute | solution.py:38
  60.4 7.6 %collective-permute-start.15 = (bf16[256,256]{1,0:T(8,128)(2,1)S(1)}, bf16[256,256]{1,0:T(8,128)(2,1)S(1)}, u32[]{:S(2)}, u32[]{:S(2)}) collective-permute-start(bf16[256,256]{1,0:T(8,128)(2,1)S(1)} %pad_maximum_fusion), channel_id=1, source_target_pairs={{0,8},{4,12},{8,0},{12,4},{16,24},{20,28},{24,16},{28,20},{1,9},{5... | collective-permute-start | bytes 393224 | tf_op jit(solution)/shard_map/ppermute | solution.py:38
  61.0 7.4 %collective-permute-start.16 = (bf16[256,256]{1,0:T(8,128)(2,1)S(1)}, bf16[256,256]{1,0:T(8,128)(2,1)S(1)}, u32[]{:S(2)}, u32[]{:S(2)}) collective-permute-start(bf16[256,256]{1,0:T(8,128)(2,1)S(1)} %pad_maximum_fusion), channel_id=1, source_target_pairs={{0,16},{4,20},{8,24},{12,28},{16,0},{20,4},{24,8},{28,12},{1,17},{... | collective-permute-start | bytes 393224 | tf_op jit(solution)/shard_map/ppermute | solution.py:38
  62.5 7.5 %collective-permute-start.17 = (bf16[256,256]{1,0:T(8,128)(2,1)S(1)}, bf16[256,256]{1,0:T(8,128)(2,1)S(1)}, u32[]{:S(2)}, u32[]{:S(2)}) collective-permute-start(bf16[256,256]{1,0:T(8,128)(2,1)S(1)} %pad_maximum_fusion), channel_id=1, source_target_pairs={{0,24},{4,28},{8,16},{12,20},{16,8},{20,12},{24,0},{28,4},{1,25},{... | collective-permute-start | bytes 393224 | tf_op jit(solution)/shard_map/ppermute | solution.py:38
  67.8 27.0 %copy-start = (bf16[128,2048]{1,0:T(8,128)(2,1)S(1)}, bf16[128,2048]{1,0:T(8,128)(2,1)}, u32[]{:S(2)}) copy-start(bf16[128,2048]{1,0:T(8,128)(2,1)} %key_ref.3) | copy-start | bytes 1572868
  67.8 27.0 %copy-start.1 = (bf16[128,2048]{1,0:T(8,128)(2,1)S(1)}, bf16[128,2048]{1,0:T(8,128)(2,1)}, u32[]{:S(2)}) copy-start(bf16[128,2048]{1,0:T(8,128)(2,1)} %value_ref.3) | copy-start | bytes 1572868
  67.8 27.0 %copy-start.3 = (bf16[128,2048]{1,0:T(8,128)(2,1)S(1)}, bf16[128,2048]{1,0:T(8,128)(2,1)}, u32[]{:S(2)}) copy-start(bf16[128,2048]{1,0:T(8,128)(2,1)} %query_ref.5) | copy-start | bytes 1572868
  67.8 27.0 %copy-start.4 = (f32[128,16]{0,1:T(8,128)S(1)}, f32[128,16]{0,1:T(8,128)}, u32[]{:S(2)}) copy-start(f32[128,16]{0,1:T(8,128)} %param.16) | copy-start | bytes 24580
  67.9 27.0 %copy-start.5 = (f32[2048]{0:T(1024)S(1)}, f32[2048]{0:T(1024)}, u32[]{:S(2)}) copy-start(f32[2048]{0:T(1024)} %param.17) | copy-start | bytes 24580
  67.9 30.6 %copy-start.7 = (s32[6,2]{0,1:T(2,128)S(1)}, s32[6,2]{0,1:T(2,128)}, u32[]{:S(2)}) copy-start(s32[6,2]{0,1:T(2,128)} %param.19) | copy-start | bytes 148
  67.9 30.6 %copy-start.8 = (f32[6,2]{0,1:T(2,128)S(1)}, f32[6,2]{0,1:T(2,128)}, u32[]{:S(2)}) copy-start(f32[6,2]{0,1:T(2,128)} %param.20) | copy-start | bytes 148
  70.2 7.5 %collective-permute-start.18 = (bf16[1024,256]{1,0:T(8,128)(2,1)S(1)}, bf16[1024,256]{1,0:T(8,128)(2,1)S(1)}, u32[]{:S(2)}, u32[]{:S(2)}) collective-permute-start(bf16[1024,256]{1,0:T(8,128)(2,1)S(1)} %constant_dynamic-update-slice_fusion.7.refs_0_), channel_id=1, source_target_pairs={{0,4},{4,0},{8,12},{12,8},{16,20},{20,16},{24,28},{28,24},{1,5},{5... | collective-permute-start | bytes 1572872 | tf_op jit(solution)/shard_map/ppermute | solution.py:38
  70.2 17.6 %collective-permute-start.23 = (bf16[8,136,128]{2,1,0:T(8,128)(2,1)S(1)}, bf16[8,136,128]{2,1,0:T(8,128)(2,1)S(1)}, u32[]{:S(2)}, u32[]{:S(2)}) collective-permute-start(bf16[8,136,128]{2,1,0:T(8,128)(2,1)S(1)} %get-tuple-element.107), channel_id=1, source_target_pairs={{0,16},{4,20},{8,24},{12,28},{16,0},{20,4},{24,8},{28,12},{1,17},{... | collective-permute-start | bytes 835592 | tf_op jit(solution)/shard_map/ppermute | solution.py:38
  71.1 9.7 %collective-permute-start.12 = (bf16[32,3072]{1,0:T(8,128)(2,1)S(1)}, bf16[32,3072]{1,0:T(8,128)(2,1)S(1)}, u32[]{:S(2)}, u32[]{:S(2)}) collective-permute-start(bf16[32,3072]{1,0:T(8,128)(2,1)S(1)} %get-tuple-element.114), channel_id=1, source_target_pairs={{0,8},{4,12},{8,0},{12,4},{16,24},{20,28},{24,16},{28,20},{1,9},{5... | collective-permute-start | bytes 589832 | tf_op jit(solution)/shard_map/ppermute | solution.py:38
  72.6 15.1 %collective-permute-start.13 = (bf16[32,3072]{1,0:T(8,128)(2,1)S(1)}, bf16[32,3072]{1,0:T(8,128)(2,1)S(1)}, u32[]{:S(2)}, u32[]{:S(2)}) collective-permute-start(bf16[32,3072]{1,0:T(8,128)(2,1)S(1)} %get-tuple-element.115), channel_id=1, source_target_pairs={{0,16},{4,20},{8,24},{12,28},{16,0},{20,4},{24,8},{28,12},{1,17},{... | collective-permute-start | bytes 589832 | tf_op jit(solution)/shard_map/ppermute | solution.py:38
  73.1 14.6 %collective-permute-start.14 = (bf16[32,3072]{1,0:T(8,128)(2,1)S(1)}, bf16[32,3072]{1,0:T(8,128)(2,1)S(1)}, u32[]{:S(2)}, u32[]{:S(2)}) collective-permute-start(bf16[32,3072]{1,0:T(8,128)(2,1)S(1)} %get-tuple-element.116), channel_id=1, source_target_pairs={{0,24},{4,28},{8,16},{12,20},{16,8},{20,12},{24,0},{28,4},{1,25},{... | collective-permute-start | bytes 589832 | tf_op jit(solution)/shard_map/ppermute | solution.py:38
  88.6 6.2 %collective-permute-start.24 = (bf16[8,128,128]{2,1,0:T(8,128)(2,1)S(1)}, bf16[8,128,128]{2,1,0:T(8,128)(2,1)S(1)}, u32[]{:S(2)}, u32[]{:S(2)}) collective-permute-start(bf16[8,128,128]{2,1,0:T(8,128)(2,1)S(1)} %get-tuple-element.138), channel_id=1, source_target_pairs={{0,4},{4,0},{8,12},{12,8},{16,20},{20,16},{24,28},{28,24},{1,5},{5... | collective-permute-start | bytes 786440 | tf_op jit(solution)/shard_map/ppermute | solution.py:38
  88.7 1.7 %collective-permute-start.19 = (bf16[16,3072]{1,0:T(8,128)(2,1)S(1)}, bf16[16,3072]{1,0:T(8,128)(2,1)S(1)}, u32[]{:S(2)}, u32[]{:S(2)}) collective-permute-start(bf16[16,3072]{1,0:T(8,128)(2,1)S(1)} %get-tuple-element.128), channel_id=1, source_target_pairs={{0,4},{4,0},{8,12},{12,8},{16,20},{20,16},{24,28},{28,24},{1,5},{5... | collective-permute-start | bytes 294920 | tf_op jit(solution)/shard_map/ppermute | solution.py:38
  90.3 8.1 %collective-permute-start.20 = (bf16[4,6144]{1,0:T(4,128)(2,1)S(1)}, bf16[4,6144]{1,0:T(4,128)(2,1)S(1)}, u32[]{:S(2)}, u32[]{:S(2)}) collective-permute-start(bf16[4,6144]{1,0:T(4,128)(2,1)S(1)} %get-tuple-element.130), channel_id=1, source_target_pairs={{0,1},{1,0},{2,3},{3,2},{4,5},{5,4},{6,7},{7,6},{8,9},{9,8},{10,11... | collective-permute-start | bytes 147464 | tf_op jit(solution)/shard_map/ppermute | solution.py:38
  90.4 8.0 %collective-permute-start.21 = (bf16[4,6144]{1,0:T(4,128)(2,1)S(1)}, bf16[4,6144]{1,0:T(4,128)(2,1)S(1)}, u32[]{:S(2)}, u32[]{:S(2)}) collective-permute-start(bf16[4,6144]{1,0:T(4,128)(2,1)S(1)} %get-tuple-element.131), channel_id=1, source_target_pairs={{0,2},{1,3},{2,0},{3,1},{4,6},{5,7},{6,4},{7,5},{8,10},{9,11},{10,... | collective-permute-start | bytes 147464 | tf_op jit(solution)/shard_map/ppermute | solution.py:38
  92.3 6.2 %collective-permute-start.22 = (bf16[4,6144]{1,0:T(4,128)(2,1)S(1)}, bf16[4,6144]{1,0:T(4,128)(2,1)S(1)}, u32[]{:S(2)}, u32[]{:S(2)}) collective-permute-start(bf16[4,6144]{1,0:T(4,128)(2,1)S(1)} %get-tuple-element.132), channel_id=1, source_target_pairs={{0,3},{1,2},{2,1},{3,0},{4,7},{5,6},{6,5},{7,4},{8,11},{9,10},{10,... | collective-permute-start | bytes 147464 | tf_op jit(solution)/shard_map/ppermute | solution.py:38
  (2 other events, 11.3 us)
where the time goes:
time: 100 us
  Pallas kernels  55.3 us (55%)
  starting transfers between devices  24.6 us (25%)
  waiting for transfers between devices  17.3 us (17%)
  local copies, waits for them, and re-layouts  1.81 us (2%)
  between operations  1.04 us (1%)
    ppermute x25, starting transfers between devices, swap(): lax.ppermute(value, axis, [(i, i ^ offset) for i in range(lax.axis_size(a...  24.6 us
    pallas_call x2, Pallas kernels, gate_and_up(): pl.pallas_call(kernel, in_specs=[smem_spec, vmem_spec, vmem_spec, hbm_spe...  18.6 us
    ppermute x25, waiting for transfers between devices, swap(): lax.ppermute(value, axis, [(i, i ^ offset) for i in range(lax.axis_size(a...  17.3 us
    pallas_call x1, Pallas kernels, local_states(): pl.pallas_call(kernel, grid_spec=pltpu.PrefetchScalarGridSpec(num_scalar_...  11.1 us
    pallas_call x2, Pallas kernels, down(): pl.pallas_call(kernel, in_specs=[smem_spec, vmem_spec, vmem_spec, hbm_spe...  9.76 us
    pallas_call x2, Pallas kernels, softmax_layer(): pl.pallas_call(kernel, grid_spec=pltpu.PrefetchScalarGridSpec(num_scalar_...  6.19 us
    pallas_call x1, Pallas kernels, lightning(): pl.pallas_call(kernel, grid_spec=pltpu.PrefetchScalarGridSpec(num_scalar_...  3.63 us
  transfers between devices with their start and end apart: 25, of which 7 were waited for; matrix products, arithmetic and copies ran while one was open for 0% of the time, Pallas kernels for 44%

commit v1 on v0

--- a/solution.py
+++ b/solution.py
@@ -84,7 +84,7 @@
         out_specs=[vmem_spec] * planes,
         out_shape=[shape((each, width), BF16)] * planes,
         compiler_params=params(2),
-    )(flags, routes.T, *in_hbm(moe_input))
+    )(flags, *in_hbm(routes.T, moe_input))
 
 
 def arrange(arrived):
@@ -146,9 +146,24 @@
     return max(d for d in range(unit, most + 1, unit) if total % d == 0)
 
 
-def gate_and_up(flags, which, x_half, gate_half, up_weight, sums=None, down_weight=None):
+PIECES = 2
+
+
+def copies(source, target, sems):
+    rows = target.shape[0]
+    pieces = max(p for p in range(1, PIECES + 1) if rows % (8 * p) == 0)
+    each = rows // pieces
+    return [
+        pltpu.make_async_copy(
+            source.at[c * each : (c + 1) * each], target.at[c * each : (c + 1) * each], sems.at[c]
+        )
+        for c in range(pieces)
+    ]
+
+
+def gate_and_up(flags, which, x_half, gates, up_weight, sums=None, down_weight=None):
     rows, part = x_half.shape
-    experts, _, hidden = gate_half.shape
+    experts, _, hidden = up_weight.shape
     deep = divisor(part, 1536)
     chunks = part // deep
     final = sums is not None
@@ -158,7 +173,8 @@
     blocks = lax.axis_size("ctx")
     block = rows // blocks
 
-    def kernel(flags_ref, x_ref, gate_ref, up_ref, *refs):
+    def kernel(flags_ref, x_ref, *refs):
+        gate_refs, up_ref, refs = refs[: len(gates)], refs[len(gates)], refs[len(gates) + 1 :]
         if final:
             (gate_in, up_in, up_first, down_ref, inner_ref, early_ref,
              ups, sems, early_sems, x_held) = refs
@@ -175,8 +191,9 @@
                 fetch(e, s).start()
         if not final:
             rest = pl.ds(pl.multiple_of((1 - half) * part, part), part)
-            following = pltpu.make_async_copy(up_ref.at[0, rest], next_ref, next_sem)
-            following.start()
+            following = copies(up_ref.at[0, rest], next_ref, next_sem)
+            for copy in following:
+                copy.start()
         if final:
             early = fetch_ahead(flags_ref[1] ^ 1, part, ahead, down_ref, early_ref, early_sems)
             for copy in early:
@@ -184,35 +201,43 @@
             expert_of = lax.rem(
                 lax.div(lax.broadcasted_iota(jnp.int32, (rows, 1), 0), CAP), experts
             )
-        if final:
-            for k in range(blocks):
-                x_held[k * block : (k + 1) * block] = x_ref[(k ^ 1) * block : ((k ^ 1) + 1) * block]
-            x_ref = x_held
-        for e in range(experts):
-            gate = jnp.dot(x_ref[...], gate_ref[e], preferred_element_type=F32)
+
+        @pl.when(flags_ref[0] >= 0)
+        def _():
+            x_used = x_ref
             if final:
-                gate_in[e] = gate_in[e] + gate
+                for k in range(blocks):
+                    x_held[k * block : (k + 1) * block] = x_ref[(k ^ 1) * block : ((k ^ 1) + 1) * block]
+                x_used = x_held
+            for e in range(experts):
+                if len(gate_refs[0].shape) == 3:
+                    weight = gate_refs[0][e]
+                else:
+                    weight = gate_refs[0][...] if e == 0 else gate_refs[1][e - 1]
+                gate = jnp.dot(x_used[...], weight, preferred_element_type=F32)
+                if final:
+                    gated = gate_in[e] + gate
+                else:
+                    gate_out[e] = gate
+                if e < given:
+                    weight = up_first[...]
+                else:
+                    for s in range(chunks):
+                        fetch(e, s).wait()
+                    weight = ups[e - given].reshape(part, hidden)
+                up = jnp.dot(x_used[...], weight, preferred_element_type=F32)
+                if final:
+                    value = gated / (1.0 + jnp.exp(-gated)) * (up_in[e] + up)
+                    here = jnp.broadcast_to(expert_of, (rows, hidden)) == e
+                    inner_ref[e] = jnp.where(here, value, 0.0).astype(BF16)
+                else:
+                    up_out[e] = up
+            if final:
+                for copy in early:
+                    copy.wait()
             else:
-                gate_out[e] = gate
-            if e < given:
-                weight = up_first[...]
-            else:
-                for s in range(chunks):
-                    fetch(e, s).wait()
-                weight = ups[e - given].reshape(part, hidden)
-            up = jnp.dot(x_ref[...], weight, preferred_element_type=F32)
-            if final:
-                gated = gate_in[e]
-                value = gated / (1.0 + jnp.exp(-gated)) * (up_in[e] + up)
-                here = jnp.broadcast_to(expert_of, (rows, hidden)) == e
-                inner_ref[e] = jnp.where(here, value, 0.0).astype(BF16)
-            else:
-                up_out[e] = up
-        if final:
-            for copy in early:
-                copy.wait()
-        else:
-            following.wait()
+                for copy in following:
+                    copy.wait()
 
     partial = shape((experts, rows, hidden), F32)
     scratch = [
@@ -225,22 +250,22 @@
             pltpu.VMEM((experts, hidden, ahead), BF16),
         ]
         scratch = scratch + [
-            pltpu.SemaphoreType.DMA((experts,)), pltpu.VMEM((rows, part), BF16)
+            pltpu.SemaphoreType.DMA((experts, PIECES)), pltpu.VMEM((rows, part), BF16)
         ]
         operands, specs = (*sums, *in_hbm(down_weight)), [vmem_spec] * 3 + [hbm_spec]
     else:
         out_shape = [partial, partial, pltpu.VMEM((part, hidden), BF16)]
-        scratch = scratch + [pltpu.SemaphoreType.DMA]
+        scratch = scratch + [pltpu.SemaphoreType.DMA((PIECES,))]
         operands, specs = (), []
     return pl.pallas_call(
         kernel,
-        in_specs=[smem_spec, vmem_spec, vmem_spec, hbm_spec] + specs,
+        in_specs=[smem_spec, vmem_spec] + [vmem_spec] * len(gates) + [hbm_spec] + specs,
         out_specs=[vmem_spec] * len(out_shape),
         out_shape=out_shape,
         scratch_shapes=scratch,
-        compiler_params=params(18),
+        compiler_params=params(15),
         cost_estimate=cost(4 * rows * experts * part * hidden, 4 * experts * part * hidden),
-    )(flags, x_half, gate_half, *in_hbm(up_weight), *operands)
+    )(flags, x_half, *gates, *in_hbm(up_weight), *operands)
 
 
 def down_step(part):
@@ -255,8 +280,9 @@
 def fetch_ahead(half, part, ahead, weight_ref, to_ref, sems):
     at = pl.ds(pl.multiple_of(half * part, 128), ahead)
     return [
-        pltpu.make_async_copy(weight_ref.at[e, :, at], to_ref.at[e], sems.at[e])
+        copy
         for e in range(to_ref.shape[0])
+        for copy in copies(weight_ref.at[e, :, at], to_ref.at[e], sems.at[e])
     ]
 
 
@@ -280,10 +306,11 @@
         def fetch(i):
             at = pl.ds(pl.multiple_of(half * part + i * wide, 128), wide)
             return [
-                pltpu.make_async_copy(
+                copy
+                for e in range(experts)
+                for copy in copies(
                     down_ref.at[e, :, at], downs.at[i - done, e], sems.at[i - done, e]
                 )
-                for e in range(experts)
             ]
 
         for i in range(done, steps):
@@ -293,35 +320,38 @@
             following = fetch_ahead(flags_ref[1], part, ahead, down_ref, next_ref, next_sems)
             for copy in following:
                 copy.start()
-        for i in range(steps):
-            if i >= done:
-                for copy in fetch(i):
+
+        @pl.when(flags_ref[0] >= 0)
+        def _():
+            for i in range(steps):
+                if i >= done:
+                    for copy in fetch(i):
+                        copy.wait()
+                total = None
+                for e in range(experts):
+                    weight = early_ref[e, :, i * wide : (i + 1) * wide] if i < done else downs[i - done, e]
+                    term = jnp.dot(inner_ref[e], weight, preferred_element_type=F32)
+                    total = term if total is None else total + term
+                at = slice(i * wide, (i + 1) * wide)
+                if which == 0:
+                    out_ref[:, at] = total
+                else:
+                    for k in range(rows // block):
+                        out_ref[k * block : (k + 1) * block, at] = total[
+                            (k ^ 1) * block : ((k ^ 1) + 1) * block
+                        ].astype(BF16)
+            if which == 1:
+                for copy in following:
                     copy.wait()
-            total = None
-            for e in range(experts):
-                weight = early_ref[e, :, i * wide : (i + 1) * wide] if i < done else downs[i - done, e]
-                term = jnp.dot(inner_ref[e], weight, preferred_element_type=F32)
-                total = term if total is None else total + term
-            at = slice(i * wide, (i + 1) * wide)
-            if which == 0:
-                out_ref[:, at] = total
-            else:
-                for k in range(rows // block):
-                    out_ref[k * block : (k + 1) * block, at] = total[
-                        (k ^ 1) * block : ((k ^ 1) + 1) * block
-                    ].astype(BF16)
-        if which == 1:
-            for copy in following:
-                copy.wait()
 
     scratch = [
         pltpu.VMEM((left, experts, hidden, wide), BF16),
-        pltpu.SemaphoreType.DMA((left, experts)),
+        pltpu.SemaphoreType.DMA((left, experts, PIECES)),
     ]
     out_shape = [shape((rows, part), BF16 if which == 1 else F32)]
     if which == 1:
         out_shape.append(pltpu.VMEM((experts, hidden, ahead), BF16))
-        scratch.append(pltpu.SemaphoreType.DMA((experts,)))
+        scratch.append(pltpu.SemaphoreType.DMA((experts, PIECES)))
     return pl.pallas_call(
         kernel,
         in_specs=[smem_spec, vmem_spec, vmem_spec, hbm_spec],
@@ -424,30 +454,47 @@
     return state, tail[0:1] + tail[1:2]
 
 
+def fetch_gate(flags, gate_weight):
+    _, width, hidden = gate_weight.shape
+    part = width // 2
+
+    def kernel(flags_ref, gate_ref, out_ref, sems):
+        at = pl.ds(pl.multiple_of(flags_ref[1] * part, part), part)
+        under_way = copies(gate_ref.at[0, at], out_ref, sems)
+        for copy in under_way:
+            copy.start()
+        for copy in under_way:
+            copy.wait()
+
+    return pl.pallas_call(
+        kernel,
+        in_specs=[smem_spec, hbm_spec],
+        out_specs=vmem_spec,
+        out_shape=pltpu.VMEM((part, hidden), BF16),
+        scratch_shapes=[pltpu.SemaphoreType.DMA((PIECES,))],
+        compiler_params=params(2),
+        cost_estimate=cost(0, 2 * part * hidden),
+    )(flags, *in_hbm(gate_weight))
+
+
 def local_states(flags, lin_key, lin_value, log_decay, gate_weight):
     length, heads = log_decay.shape
     size = lin_key.shape[1] // heads
     half = heads // 2
     experts, width, hidden = gate_weight.shape
     part = width // 2
-    chunks = 2
+    counts = [experts] + ([experts - 1] if experts > 1 else [])
 
     def kernel(flags_ref, key_ref, value_ref, decay_ref, gate_ref, mine_ref, factor_ref, send_ref,
-               own_gate, other_gate, sems):
+               *refs):
+        *gate_outs, sems = refs
         step = pl.program_id(0)
 
         def fetch():
-            for h, to in enumerate((own_gate, other_gate)):
-                for e in range(experts):
-                    for c in range(chunks):
-                        rows = part // chunks
-                        at = pl.ds(
-                            pl.multiple_of((flags_ref[1] ^ h) * part + c * rows, rows), rows
-                        )
-                        yield pltpu.make_async_copy(
-                            gate_ref.at[e, at], to.at[e, c * rows : (c + 1) * rows],
-                            sems.at[h, e, c],
-                        )
+            for h, to in zip((1, 0), gate_outs):
+                at = pl.ds(pl.multiple_of((flags_ref[1] ^ h) * part, part), part)
+                for e in range(1 - h, experts):
+                    yield from copies(gate_ref.at[e, at], to.at[e - (1 - h)], sems.at[h, e])
 
         @pl.when(step == 0)
         def _():
@@ -494,19 +541,17 @@
                 full((half, size, size)),
                 full((half, size)),
                 full((half, size + EXTRA, size)),
-                vmem_spec,
-                vmem_spec,
-            ],
-            scratch_shapes=[pltpu.SemaphoreType.DMA((2, experts, chunks))],
+            ]
+            + [vmem_spec] * len(counts),
+            scratch_shapes=[pltpu.SemaphoreType.DMA((2, experts, PIECES))],
         ),
         out_shape=[
             shape((half, size, size), F32),
             shape((half, size), F32),
             shape((half, size + EXTRA, size), BF16),
-            pltpu.VMEM((experts, part, hidden), BF16),
-            pltpu.VMEM((experts, part, hidden), BF16),
-        ],
-        compiler_params=params(8),
+        ]
+        + [pltpu.VMEM((one, part, hidden), BF16) for one in counts],
+        compiler_params=params(3),
         cost_estimate=cost(
             4 * heads * length * size * size,
             4 * length * heads * size + 2 * experts * width * hidden,
@@ -755,24 +800,24 @@
     kv_width = groups * 2 * size
     after = lambda value: tie(flags, value)[0]
 
+    outgoing = pack(flags, moe_input, routes, planes, experts)
+    soft_kv = tie(soft_kv, outgoing[0])[0]
     held = soft_kv.reshape(soft_kv.shape[0], kv_width)
     kv_other = held
     if split:
         odd = flags[1] == 1
         first, second = held[:, : kv_width // 2], held[:, kv_width // 2 :]
         held, kv_other = jnp.where(odd, second, first), jnp.where(odd, first, second)
-
-    outgoing = pack(tie(flags, held)[0], moe_input, routes, planes, experts)
     arrived = [outgoing[0]] + [swap(outgoing[p], "exp", p) for p in range(1, planes)]
-    kv_other = tie(kv_other, outgoing[0])[0]
     held = jnp.concatenate([held, swap(kv_other, "ctx", 1)])
     kv_got = [swap(held, "ctx", j) for j in chips]
-    *arrived, held = tie(*arrived, held)
+    gate_first = fetch_gate(after(held), gate_weight)
+    *arrived, held, gate_first = tie(*arrived, held, gate_first)
 
     own, other = arrange(arrived)
     rows = jnp.concatenate([own, swap(other, "ctx", 1)])
     got = [swap(rows, "ctx", j) for j in chips]
-    mine, factor, message, own_gate, other_gate = local_states(
+    mine, factor, message, other_gate, *own_rest = local_states(
         after(rows), lin_key, lin_value, log_decay, gate_weight
     )
     *got, message = tie(*got, message)
@@ -780,14 +825,14 @@
     far = swap(near, "ctx", 1)
     neighbour = swap(message, "ctx", 1)
 
-    sums = gate_and_up(flags, 0, near, own_gate, up_weight)
+    sums = gate_and_up(flags, 0, near, [gate_first, *own_rest], up_weight)
     total, total_factor, message = join_pair(after(sums[0]), mine, factor, neighbour)
     far, message = tie(far, message)
     before = before_factor = got = None
     if high:
         got = swap(message, "ctx", 2)
     inner, early = gate_and_up(
-        flags, 1, far, other_gate, up_weight, sums, down_weight
+        flags, 1, far, [other_gate], up_weight, sums, down_weight
     )
     for i, b in enumerate(high[:-1]):
         total, total_factor, message, before, before_factor = join_group(

time: 100 us -> 94.2 us (0.942)
  waiting for transfers between devices: 17.3 us -> 13.5 us
  Pallas kernels: 55.3 us -> 52.9 us
    ppermute x25, waiting for transfers between devices: 17.3 us -> 13.5 us  [swap(): lax.ppermute(value, axis, [(i, i ^ offset) for i in range(lax.axis_size(a...]
    pallas_call x1, Pallas kernels: 11.1 us -> 8.84 us  [local_states(): pl.pallas_call(kernel, grid_spec=pltpu.PrefetchScalarGridSpec(num_scalar_...]
    pallas_call x2 -> x3, Pallas kernels: 18.6 us -> 18.5 us  [the longest x2 14.9 us: gate_and_up(): pl.pallas_call(kernel, in_specs=[smem_spec, vmem_spec] + [vmem_spec] * le...]
  transfers between devices with their start and end apart: 25 -> 25, of which waited for: 7 -> 7; matrix products, arithmetic and copies ran while one was open for 0% -> 0% of each run, Pallas kernels for 44% -> 45%
where the time goes in v1:
time: 94.2 us; the launch traced here: 94 us
  Pallas kernels  52.9 us (56%)
  starting transfers between devices  25.3 us (27%)
  waiting for transfers between devices  13.5 us (14%)
  local copies, waits for them, and re-layouts  1.13 us (1%)
  between operations  1.02 us (1%)
    ppermute x25, starting transfers between devices, swap(): lax.ppermute(value, axis, [(i, i ^ offset) for i in range(lax.axis_size(a...  25.3 us
    pallas_call x2, Pallas kernels, gate_and_up(): pl.pallas_call(kernel, in_specs=[smem_spec, vmem_spec] + [vmem_spec] * le...  14.9 us
    ppermute x25, waiting for transfers between devices, swap(): lax.ppermute(value, axis, [(i, i ^ offset) for i in range(lax.axis_size(a...  13.5 us
    pallas_call x2, Pallas kernels, down(): pl.pallas_call(kernel, in_specs=[smem_spec, vmem_spec, vmem_spec, hbm_spe...  9.67 us
    pallas_call x1, Pallas kernels, local_states(): pl.pallas_call(kernel, grid_spec=pltpu.PrefetchScalarGridSpec(num_scalar_...  8.84 us
    pallas_call x2, Pallas kernels, softmax_layer(): pl.pallas_call(kernel, grid_spec=pltpu.PrefetchScalarGridSpec(num_scalar_...  6.19 us
    pallas_call x1, Pallas kernels, fetch_gate(): pl.pallas_call(kernel, in_specs=[smem_spec, hbm_spec], out_specs=vmem_spe...  3.64 us
    pallas_call x1, Pallas kernels, lightning(): pl.pallas_call(kernel, grid_spec=pltpu.PrefetchScalarGridSpec(num_scalar_...  3.63 us
  transfers between devices with their start and end apart: 25, of which 7 were waited for; matrix products, arithmetic and copies ran while one was open for 0% of the time, Pallas kernels for 45%

profile of v1, /device:TPU:0, one launch (start us, length us, event | category | flops | bytes accessed | tf_op | source)
XLA Modules:
  0.0 94.0 jit_solution(15206899127924876483)
XLA Ops:
  0.7 1.2 %shard_map.148 = (bf16[4,6144]{1,0:T(4,128)(2,1)S(1)}, bf16[4,6144]{1,0:T(4,128)(2,1)S(1)}, bf16[4,6144]{1,0:T(4,128)(2,1)S(1)}, bf16[4,6144]{1,0:T(4,128)(2,1)S(1)}) custom-call(s32[3]{0:T(128)S(1)} %pad_add_fusion.flags_ref, s32[2,6]{1,0:T(2,128)} %bitcast.10, bf16[6,6144]{1,0:T(8,128)(2,1)} %x_ref.1), custom_call_target="tpu_custom_call" | custom-call | tf_op jit(solution)/shard_map/pallas_call | solution.py:81
  1.9 1.0 %reshape.12 = bf16[128,512]{1,0:T(8,128)(2,1)S(1)} reshape(bf16[128,2,2,128]{3,2,1,0:T(2,128)(2,1)} %param.25) | data formatting | bytes 262144 | tf_op jit(solution)/shard_map/reshape | solution.py:805
  3.5 2.6 %collective-permute-start = (bf16[4,6144]{1,0:T(4,128)(2,1)S(1)}, bf16[4,6144]{1,0:T(4,128)(2,1)S(1)}, u32[]{:S(2)}, u32[]{:S(2)}) collective-permute-start(bf16[4,6144]{1,0:T(4,128)(2,1)S(1)} %get-tuple-element.76), channel_id=1, source_target_pairs={{0,1},{1,0},{2,3},{3,2},{4,5},{5,4},{6,7},{7,6},{8,9},{9,8},{10,11... | collective-permute-start | bytes 147464 | tf_op jit(solution)/shard_map/ppermute | solution.py:38
  6.1 2.6 %collective-permute-start.1 = (bf16[4,6144]{1,0:T(4,128)(2,1)S(1)}, bf16[4,6144]{1,0:T(4,128)(2,1)S(1)}, u32[]{:S(2)}, u32[]{:S(2)}) collective-permute-start(bf16[4,6144]{1,0:T(4,128)(2,1)S(1)} %get-tuple-element.77), channel_id=1, source_target_pairs={{0,2},{1,3},{2,0},{3,1},{4,6},{5,7},{6,4},{7,5},{8,10},{9,11},{10,... | collective-permute-start | bytes 147464 | tf_op jit(solution)/shard_map/ppermute | solution.py:38
  8.7 3.6 %shard_map.149.refs_0_ = bf16[3072,1152]{1,0:T(8,128)(2,1)S(1)} custom-call(s32[3]{0:T(128)S(1)} %pad_add_fusion.flags_ref, bf16[2,6144,1152]{2,1,0:T(8,128)(2,1)} %gate_ref.3), custom_call_target="tpu_custom_call" | custom-call | bytes 7077888 | tf_op jit(solution)/shard_map/pallas_call | solution.py:469
  12.4 2.2 %collective-permute-done.2.refs_3_ = bf16[4,6144]{1,0:T(4,128)(2,1)S(1)} collective-permute-done((bf16[4,6144]{1,0:T(4,128)(2,1)S(1)}, bf16[4,6144]{1,0:T(4,128)(2,1)S(1)}, u32[]{:S(2)}, u32[]{:S(2)}) %collective-permute-start.2) | collective-permute-done | bytes 49184 | tf_op jit(solution)/shard_map/ppermute | solution.py:38
  14.7 1.3 %collective-permute-done.4 = bf16[16,3072]{1,0:T(8,128)(2,1)S(1)} collective-permute-done((bf16[16,3072]{1,0:T(8,128)(2,1)S(1)}, bf16[16,3072]{1,0:T(8,128)(2,1)S(1)}, u32[]{:S(2)}, u32[]{:S(2)}) %collective-permute-start.4) | collective-permute-done | bytes 98336 | tf_op jit(solution)/shard_map/ppermute | solution.py:38
  16.0 1.6 %collective-permute-start.5 = (bf16[32,3072]{1,0:T(8,128)(2,1)S(1)}, bf16[32,3072]{1,0:T(8,128)(2,1)S(1)}, u32[]{:S(2)}, u32[]{:S(2)}) collective-permute-start(bf16[32,3072]{1,0:T(8,128)(2,1)S(1)} %get-tuple-element.149), channel_id=1, source_target_pairs={{0,8},{4,12},{8,0},{12,4},{16,24},{20,28},{24,16},{28,20},{1,9},{5... | collective-permute-start | bytes 589832 | tf_op jit(solution)/shard_map/ppermute | solution.py:38
  17.6 1.5 %collective-permute-start.6 = (bf16[32,3072]{1,0:T(8,128)(2,1)S(1)}, bf16[32,3072]{1,0:T(8,128)(2,1)S(1)}, u32[]{:S(2)}, u32[]{:S(2)}) collective-permute-start(bf16[32,3072]{1,0:T(8,128)(2,1)S(1)} %get-tuple-element.149), channel_id=1, source_target_pairs={{0,16},{4,20},{8,24},{12,28},{16,0},{20,4},{24,8},{28,12},{1,17},{... | collective-permute-start | bytes 589832 | tf_op jit(solution)/shard_map/ppermute | solution.py:38
  19.6 8.8 %shard_map.151 = (f32[8,128,128]{2,1,0:T(8,128)S(1)}, f32[8,128]{1,0:T(8,128)S(1)}, bf16[8,136,128]{2,1,0:T(8,128)(2,1)S(1)}, bf16[2,3072,1152]{2,1,0:T(8,128)(2,1)S(1)}, bf16[1,3072,1152]{2,1,0:T(8,128)(2,1)S(1)}) custom-call(s32[3]{0:T(128)S(1)} %pad_add_fusion.flags_ref, bf16[128,2048]{1,0:T(8,128)(2,1)} %key_ref.3, bf16[128,2048]{1,0:T(8,128)(2,1)} %value_ref.3, ...), custom_call_target="tpu_custom_call" | custom-call | flops 134217728 | bytes 29360128 | tf_op jit(solution)/shard_map/pallas_call | solution.py:534
  29.1 7.9 %shard_map.152 = (f32[2,128,1152]{2,1,0:T(8,128)S(1)}, f32[2,128,1152]{2,1,0:T(8,128)S(1)}, bf16[3072,1152]{1,0:T(8,128)(2,1)S(1)}) custom-call(s32[3]{0:T(128)S(1)} %pad_add_fusion.flags_ref, bf16[128,3072]{1,0:T(8,128)(2,1)S(1)} %constant_dynamic-update-slice_fusion.2.x_ref, bf16[3072,1152]{1,0:T(8,128)(2,1)S(1)} %shard_map.149.refs_0_, ...), custom_call_target="tpu_custom_call" | custom-call | flops 3623878656 | bytes 28311552 | tf_op jit(solution)/shard_map/pallas_call | solution.py:260
  37.0 0.7 shard_map.153
  37.7 1.5 %collective-permute-start.10 = (bf16[8,136,128]{2,1,0:T(8,128)(2,1)S(1)}, bf16[8,136,128]{2,1,0:T(8,128)(2,1)S(1)}, u32[]{:S(2)}, u32[]{:S(2)}) collective-permute-start(bf16[8,136,128]{2,1,0:T(8,128)(2,1)S(1)} %get-tuple-element.108), channel_id=1, source_target_pairs={{0,8},{4,12},{8,0},{12,4},{16,24},{20,28},{24,16},{28,20},{1,9},{5... | collective-permute-start | bytes 835592 | tf_op jit(solution)/shard_map/ppermute | solution.py:38
  39.3 7.0 %shard_map.154 = (bf16[2,128,1152]{2,1,0:T(8,128)(2,1)S(1)}, bf16[2,1152,2048]{2,1,0:T(8,128)(2,1)S(1)}) custom-call(s32[3]{0:T(128)S(1)} %pad_add_fusion.flags_ref, bf16[128,3072]{1,0:T(8,128)(2,1)S(1)} %collective-permute-done.8.x_ref, bf16[2,3072,1152]{2,1,0:T(8,128)(2,1)S(1)} %get-tuple-element.101.refs_0_, bf16[2,6144,1152]{2,1,0:T(8,128)(2,1)} %refs_1_.1, ...), custom_call_target="tpu_custom_call" | custom-call | flops 3623878656 | bytes 28311552 | tf_op jit(solution)/shard_map/pallas_call | solution.py:260
  46.4 1.5 %shard_map.155 = (f32[8,128,128]{2,1,0:T(8,128)}, f32[8,128]{1,0:T(8,128)}, bf16[8,136,128]{2,1,0:T(8,128)(2,1)S(1)}, f32[8,128,128]{2,1,0:T(8,128)S(1)}, f32[8,128]{1,0:T(8,128)S(1)}) custom-call(s32[3]{0:T(128)S(1)} %pad_add_fusion.flags_ref, f32[8,128,128]{2,1,0:T(8,128)S(1)} %get-tuple-element.106.total_ref, f32[8,128]{1,0:T(8,128)S(1)} %get-tuple-element.107.factor_ref, ...), custom_call_target="tpu_custom_call" | custom-call | tf_op jit(solution)/shard_map/pallas_call | solution.py:618
  47.9 5.9 %shard_map.156 = (bf16[128,3072]{1,0:T(8,128)(2,1)S(1)}, bf16[2,1152,2048]{2,1,0:T(8,128)(2,1)S(1)}) custom-call(s32[3]{0:T(128)S(1)} %pad_add_fusion.flags_ref, bf16[2,128,1152]{2,1,0:T(8,128)(2,1)S(1)} %get-tuple-element.110.inner_ref, bf16[2,1152,2048]{2,1,0:T(8,128)(2,1)S(1)} %get-tuple-element.111.early_ref, bf16[2,1152,6144]{2,1,0:T(8,128)(2,1)} %down_ref.3), custom_call_target="tpu_custom_call" | custom-call | flops 1811939328 | bytes 14155776 | tf_op jit(solution)/shard_map/pallas_call | solution.py:355
  53.9 1.5 %collective-permute-start.15 = (bf16[256,256]{1,0:T(8,128)(2,1)S(1)}, bf16[256,256]{1,0:T(8,128)(2,1)S(1)}, u32[]{:S(2)}, u32[]{:S(2)}) collective-permute-start(bf16[256,256]{1,0:T(8,128)(2,1)S(1)} %pad_maximum_fusion), channel_id=1, source_target_pairs={{0,8},{4,12},{8,0},{12,4},{16,24},{20,28},{24,16},{28,20},{1,9},{5... | collective-permute-start | bytes 393224 | tf_op jit(solution)/shard_map/ppermute | solution.py:38
  55.4 1.5 %collective-permute-start.16 = (bf16[256,256]{1,0:T(8,128)(2,1)S(1)}, bf16[256,256]{1,0:T(8,128)(2,1)S(1)}, u32[]{:S(2)}, u32[]{:S(2)}) collective-permute-start(bf16[256,256]{1,0:T(8,128)(2,1)S(1)} %pad_maximum_fusion), channel_id=1, source_target_pairs={{0,16},{4,20},{8,24},{12,28},{16,0},{20,4},{24,8},{28,12},{1,17},{... | collective-permute-start | bytes 393224 | tf_op jit(solution)/shard_map/ppermute | solution.py:38
  57.4 3.8 %shard_map.157.keep_ref = f32[128,3072]{1,0:T(8,128)S(1)} custom-call(s32[3]{0:T(128)S(1)} %pad_add_fusion.flags_ref, bf16[2,128,1152]{2,1,0:T(8,128)(2,1)S(1)} %get-tuple-element.110.inner_ref, bf16[2,1152,2048]{2,1,0:T(8,128)(2,1)S(1)} %get-tuple-element.114.early_ref, bf16[2,1152,6144]{2,1,0:T(8,128)(2,1)} %down_ref.3), custom_call_target="tpu_custom_call" | custom-call | flops 1811939328 | bytes 14155776 | tf_op jit(solution)/shard_map/pallas_call | solution.py:355
  61.5 2.3 %collective-permute-done.16 = bf16[256,256]{1,0:T(8,128)(2,1)S(1)} collective-permute-done((bf16[256,256]{1,0:T(8,128)(2,1)S(1)}, bf16[256,256]{1,0:T(8,128)(2,1)S(1)}, u32[]{:S(2)}, u32[]{:S(2)}) %collective-permute-start.16) | collective-permute-done | bytes 131104 | tf_op jit(solution)/shard_map/ppermute | solution.py:38
  63.9 1.6 %collective-permute-start.23 = (bf16[8,136,128]{2,1,0:T(8,128)(2,1)S(1)}, bf16[8,136,128]{2,1,0:T(8,128)(2,1)S(1)}, u32[]{:S(2)}, u32[]{:S(2)}) collective-permute-start(bf16[8,136,128]{2,1,0:T(8,128)(2,1)S(1)} %get-tuple-element.109), channel_id=1, source_target_pairs={{0,16},{4,20},{8,24},{12,28},{16,0},{20,4},{24,8},{28,12},{1,17},{... | collective-permute-start | bytes 835592 | tf_op jit(solution)/shard_map/ppermute | solution.py:38
  66.1 1.2 %collective-permute-start.13 = (bf16[32,3072]{1,0:T(8,128)(2,1)S(1)}, bf16[32,3072]{1,0:T(8,128)(2,1)S(1)}, u32[]{:S(2)}, u32[]{:S(2)}) collective-permute-start(bf16[32,3072]{1,0:T(8,128)(2,1)S(1)} %get-tuple-element.117), channel_id=1, source_target_pairs={{0,16},{4,20},{8,24},{12,28},{16,0},{20,4},{24,8},{28,12},{1,17},{... | collective-permute-start | bytes 589832 | tf_op jit(solution)/shard_map/ppermute | solution.py:38
  67.3 1.8 %collective-permute-start.14 = (bf16[32,3072]{1,0:T(8,128)(2,1)S(1)}, bf16[32,3072]{1,0:T(8,128)(2,1)S(1)}, u32[]{:S(2)}, u32[]{:S(2)}) collective-permute-start(bf16[32,3072]{1,0:T(8,128)(2,1)S(1)} %get-tuple-element.118), channel_id=1, source_target_pairs={{0,24},{4,28},{8,16},{12,20},{16,8},{20,12},{24,0},{28,4},{1,25},{... | collective-permute-start | bytes 589832 | tf_op jit(solution)/shard_map/ppermute | solution.py:38
  69.0 3.1 %shard_map.159.refs_1_ = bf16[128,2048]{1,0:T(8,128)(2,1)} custom-call(s32[3]{0:T(128)S(1)} %pad_add_fusion.flags_ref, bf16[128,2048]{1,0:T(8,128)(2,1)S(1)} %copy-done.2, bf16[1024,256]{1,0:T(8,128)(2,1)S(1)} %constant_dynamic-update-slice_fusion.7.refs_0_), custom_call_target="tpu_custom_call" | custom-call | flops 536870912 | bytes 524288 | tf_op jit(solution)/shard_map/pallas_call | solution.py:762
  72.1 3.1 %shard_map.160 = bf16[128,2048]{1,0:T(8,128)(2,1)} custom-call(s32[3]{0:T(128)S(1)} %pad_add_fusion.flags_ref, bf16[128,2048]{1,0:T(8,128)(2,1)S(1)} %copy-done.2, bf16[1024,256]{1,0:T(8,128)(2,1)S(1)} %collective-permute-done.18.refs_0_, bf16[128,2048]{1,0:T(8,128)(2,1)} %shard_map.159.refs_1_), custom_call_target="tpu_custom_call", output_to_operand_aliasing={{}: (3, {})} | custom-call | flops 536870912 | bytes 524288 | tf_op jit(solution)/shard_map/pallas_call | solution.py:762
  75.2 6.2 %collective-permute-done.13.refs_1_ = bf16[32,3072]{1,0:T(8,128)(2,1)S(1)} collective-permute-done((bf16[32,3072]{1,0:T(8,128)(2,1)S(1)}, bf16[32,3072]{1,0:T(8,128)(2,1)S(1)}, u32[]{:S(2)}, u32[]{:S(2)}) %collective-permute-start.13) | collective-permute-done | bytes 196640 | tf_op jit(solution)/shard_map/ppermute | solution.py:38
  81.5 0.7 shard_map.163
  82.9 1.2 %collective-permute-done.19.other_ref = bf16[16,3072]{1,0:T(8,128)(2,1)S(1)} collective-permute-done((bf16[16,3072]{1,0:T(8,128)(2,1)S(1)}, bf16[16,3072]{1,0:T(8,128)(2,1)S(1)}, u32[]{:S(2)}, u32[]{:S(2)}) %collective-permute-start.19) | collective-permute-done | bytes 98336 | tf_op jit(solution)/shard_map/ppermute | solution.py:38
  84.1 2.2 %collective-permute-start.21 = (bf16[4,6144]{1,0:T(4,128)(2,1)S(1)}, bf16[4,6144]{1,0:T(4,128)(2,1)S(1)}, u32[]{:S(2)}, u32[]{:S(2)}) collective-permute-start(bf16[4,6144]{1,0:T(4,128)(2,1)S(1)} %get-tuple-element.133), channel_id=1, source_target_pairs={{0,2},{1,3},{2,0},{3,1},{4,6},{5,7},{6,4},{7,5},{8,10},{9,11},{10,... | collective-permute-start | bytes 147464 | tf_op jit(solution)/shard_map/ppermute | solution.py:38
  86.3 2.2 %collective-permute-start.22 = (bf16[4,6144]{1,0:T(4,128)(2,1)S(1)}, bf16[4,6144]{1,0:T(4,128)(2,1)S(1)}, u32[]{:S(2)}, u32[]{:S(2)}) collective-permute-start(bf16[4,6144]{1,0:T(4,128)(2,1)S(1)} %get-tuple-element.134), channel_id=1, source_target_pairs={{0,3},{1,2},{2,1},{3,0},{4,7},{5,6},{6,5},{7,4},{8,11},{9,10},{10,... | collective-permute-start | bytes 147464 | tf_op jit(solution)/shard_map/ppermute | solution.py:38
  88.5 3.6 %shard_map.164 = bf16[128,2048]{1,0:T(8,128)(2,1)} custom-call(s32[3]{0:T(128)S(1)} %pad_add_fusion.flags_ref, bf16[128,2048]{1,0:T(8,128)(2,1)S(1)} %copy-done.3, bf16[128,2048]{1,0:T(8,128)(2,1)S(1)} %copy-done, bf16[128,2048]{1,0:T(8,128)(2,1)S(1)} %copy-done.1, f32[16,128]{1,0:T(8,128)S(1)} %bitcast.8, f32[1,2048]{1,0:T(1,128)S(1)} %bitcast.9, ...), custom_call_target="tpu_custom_call" | custom-call | flops 201326592 | bytes 2097152 | tf_op jit(solution)/shard_map/pallas_call | solution.py:705
  92.3 1.7 %shard_map.165 = bf16[6,6144]{1,0:T(8,128)(2,1)} custom-call(s32[3]{0:T(128)S(1)} %pad_add_fusion.flags_ref, s32[2,6]{1,0:T(2,128)S(1)} %bitcast.11, f32[2,6]{1,0:T(2,128)S(1)} %bitcast.12, bf16[4,6144]{1,0:T(4,128)(2,1)S(1)} %get-tuple-element.142.refs_0_, bf16[4,6144]{1,0:T(4,128)(2,1)S(1)} %collective-permute-done.20.refs_1_, ...), custom_call_target="tpu_custom_call" | custom-call | tf_op jit(solution)/shard_map/pallas_call | solution.py:136
  (65 shorter events, 4.5 us)
Async XLA Ops:
  2.9 5.8 %collective-permute-start.3 = (bf16[128,256]{1,0:T(8,128)(2,1)S(1)}, bf16[128,256]{1,0:T(8,128)(2,1)S(1)}, u32[]{:S(2)}, u32[]{:S(2)}) collective-permute-start(bf16[128,256]{1,0:T(8,128)(2,1)S(1)} %get-tuple-element.148), channel_id=1, source_target_pairs={{0,4},{4,0},{8,12},{12,8},{16,20},{20,16},{24,28},{28,24},{1,5},{5... | collective-permute-start | bytes 196616 | tf_op jit(solution)/shard_map/ppermute | solution.py:38
  3.5 8.9 %collective-permute-start = (bf16[4,6144]{1,0:T(4,128)(2,1)S(1)}, bf16[4,6144]{1,0:T(4,128)(2,1)S(1)}, u32[]{:S(2)}, u32[]{:S(2)}) collective-permute-start(bf16[4,6144]{1,0:T(4,128)(2,1)S(1)} %get-tuple-element.76), channel_id=1, source_target_pairs={{0,1},{1,0},{2,3},{3,2},{4,5},{5,4},{6,7},{7,6},{8,9},{9,8},{10,11... | collective-permute-start | bytes 147464 | tf_op jit(solution)/shard_map/ppermute | solution.py:38
  6.1 6.3 %collective-permute-start.1 = (bf16[4,6144]{1,0:T(4,128)(2,1)S(1)}, bf16[4,6144]{1,0:T(4,128)(2,1)S(1)}, u32[]{:S(2)}, u32[]{:S(2)}) collective-permute-start(bf16[4,6144]{1,0:T(4,128)(2,1)S(1)} %get-tuple-element.77), channel_id=1, source_target_pairs={{0,2},{1,3},{2,0},{3,1},{4,6},{5,7},{6,4},{7,5},{8,10},{9,11},{10,... | collective-permute-start | bytes 147464 | tf_op jit(solution)/shard_map/ppermute | solution.py:38
  8.7 5.9 %collective-permute-start.2 = (bf16[4,6144]{1,0:T(4,128)(2,1)S(1)}, bf16[4,6144]{1,0:T(4,128)(2,1)S(1)}, u32[]{:S(2)}, u32[]{:S(2)}) collective-permute-start(bf16[4,6144]{1,0:T(4,128)(2,1)S(1)} %get-tuple-element.78), channel_id=1, source_target_pairs={{0,3},{1,2},{2,1},{3,0},{4,7},{5,6},{6,5},{7,4},{8,11},{9,10},{10,... | collective-permute-start | bytes 147464 | tf_op jit(solution)/shard_map/ppermute | solution.py:38
  14.6 1.4 %collective-permute-start.4 = (bf16[16,3072]{1,0:T(8,128)(2,1)S(1)}, bf16[16,3072]{1,0:T(8,128)(2,1)S(1)}, u32[]{:S(2)}, u32[]{:S(2)}) collective-permute-start(bf16[16,3072]{1,0:T(8,128)(2,1)S(1)} %get-tuple-element.86), channel_id=1, source_target_pairs={{0,4},{4,0},{8,12},{12,8},{16,20},{20,16},{24,28},{28,24},{1,5},{5... | collective-permute-start | bytes 294920 | tf_op jit(solution)/shard_map/ppermute | solution.py:38
  16.0 12.4 %collective-permute-start.5 = (bf16[32,3072]{1,0:T(8,128)(2,1)S(1)}, bf16[32,3072]{1,0:T(8,128)(2,1)S(1)}, u32[]{:S(2)}, u32[]{:S(2)}) collective-permute-start(bf16[32,3072]{1,0:T(8,128)(2,1)S(1)} %get-tuple-element.149), channel_id=1, source_target_pairs={{0,8},{4,12},{8,0},{12,4},{16,24},{20,28},{24,16},{28,20},{1,9},{5... | collective-permute-start | bytes 589832 | tf_op jit(solution)/shard_map/ppermute | solution.py:38
  17.6 10.9 %collective-permute-start.6 = (bf16[32,3072]{1,0:T(8,128)(2,1)S(1)}, bf16[32,3072]{1,0:T(8,128)(2,1)S(1)}, u32[]{:S(2)}, u32[]{:S(2)}) collective-permute-start(bf16[32,3072]{1,0:T(8,128)(2,1)S(1)} %get-tuple-element.149), channel_id=1, source_target_pairs={{0,16},{4,20},{8,24},{12,28},{16,0},{20,4},{24,8},{28,12},{1,17},{... | collective-permute-start | bytes 589832 | tf_op jit(solution)/shard_map/ppermute | solution.py:38
  19.1 9.4 %collective-permute-start.7 = (bf16[32,3072]{1,0:T(8,128)(2,1)S(1)}, bf16[32,3072]{1,0:T(8,128)(2,1)S(1)}, u32[]{:S(2)}, u32[]{:S(2)}) collective-permute-start(bf16[32,3072]{1,0:T(8,128)(2,1)S(1)} %get-tuple-element.149), channel_id=1, source_target_pairs={{0,24},{4,28},{8,16},{12,20},{16,8},{20,12},{24,0},{28,4},{1,25},{... | collective-permute-start | bytes 589832 | tf_op jit(solution)/shard_map/ppermute | solution.py:38
  28.5 9.2 %collective-permute-start.8 = (bf16[128,3072]{1,0:T(8,128)(2,1)S(1)}, bf16[128,3072]{1,0:T(8,128)(2,1)S(1)}, u32[]{:S(2)}, u32[]{:S(2)}) collective-permute-start(bf16[128,3072]{1,0:T(8,128)(2,1)S(1)} %constant_dynamic-update-slice_fusion.2.x_ref), channel_id=1, source_target_pairs={{0,4},{4,0},{8,12},{12,8},{16,20},{20,16},{24,28},{28,24},{1,5},{5... | collective-permute-start | bytes 2359304 | tf_op jit(solution)/shard_map/ppermute | solution.py:38
  28.6 8.4 %collective-permute-start.9 = (bf16[8,136,128]{2,1,0:T(8,128)(2,1)S(1)}, bf16[8,136,128]{2,1,0:T(8,128)(2,1)S(1)}, u32[]{:S(2)}, u32[]{:S(2)}) collective-permute-start(bf16[8,136,128]{2,1,0:T(8,128)(2,1)S(1)} %get-tuple-element.98), channel_id=1, source_target_pairs={{0,4},{4,0},{8,12},{12,8},{16,20},{20,16},{24,28},{28,24},{1,5},{5... | collective-permute-start | bytes 835592 | tf_op jit(solution)/shard_map/ppermute | solution.py:38
  37.7 8.7 %collective-permute-start.10 = (bf16[8,136,128]{2,1,0:T(8,128)(2,1)S(1)}, bf16[8,136,128]{2,1,0:T(8,128)(2,1)S(1)}, u32[]{:S(2)}, u32[]{:S(2)}) collective-permute-start(bf16[8,136,128]{2,1,0:T(8,128)(2,1)S(1)} %get-tuple-element.108), channel_id=1, source_target_pairs={{0,8},{4,12},{8,0},{12,4},{16,24},{20,28},{24,16},{28,20},{1,9},{5... | collective-permute-start | bytes 835592 | tf_op jit(solution)/shard_map/ppermute | solution.py:38
  53.8 7.5 %collective-permute-start.11 = (bf16[128,3072]{1,0:T(8,128)(2,1)S(1)}, bf16[128,3072]{1,0:T(8,128)(2,1)S(1)}, u32[]{:S(2)}, u32[]{:S(2)}) collective-permute-start(bf16[128,3072]{1,0:T(8,128)(2,1)S(1)} %get-tuple-element.112), channel_id=1, source_target_pairs={{0,4},{4,0},{8,12},{12,8},{16,20},{20,16},{24,28},{28,24},{1,5},{5... | collective-permute-start | bytes 2359304 | tf_op jit(solution)/shard_map/ppermute | solution.py:38
  53.9 7.6 %collective-permute-start.15 = (bf16[256,256]{1,0:T(8,128)(2,1)S(1)}, bf16[256,256]{1,0:T(8,128)(2,1)S(1)}, u32[]{:S(2)}, u32[]{:S(2)}) collective-permute-start(bf16[256,256]{1,0:T(8,128)(2,1)S(1)} %pad_maximum_fusion), channel_id=1, source_target_pairs={{0,8},{4,12},{8,0},{12,4},{16,24},{20,28},{24,16},{28,20},{1,9},{5... | collective-permute-start | bytes 393224 | tf_op jit(solution)/shard_map/ppermute | solution.py:38
  55.4 8.4 %collective-permute-start.16 = (bf16[256,256]{1,0:T(8,128)(2,1)S(1)}, bf16[256,256]{1,0:T(8,128)(2,1)S(1)}, u32[]{:S(2)}, u32[]{:S(2)}) collective-permute-start(bf16[256,256]{1,0:T(8,128)(2,1)S(1)} %pad_maximum_fusion), channel_id=1, source_target_pairs={{0,16},{4,20},{8,24},{12,28},{16,0},{20,4},{24,8},{28,12},{1,17},{... | collective-permute-start | bytes 393224 | tf_op jit(solution)/shard_map/ppermute | solution.py:38
  56.9 6.8 %collective-permute-start.17 = (bf16[256,256]{1,0:T(8,128)(2,1)S(1)}, bf16[256,256]{1,0:T(8,128)(2,1)S(1)}, u32[]{:S(2)}, u32[]{:S(2)}) collective-permute-start(bf16[256,256]{1,0:T(8,128)(2,1)S(1)} %pad_maximum_fusion), channel_id=1, source_target_pairs={{0,24},{4,28},{8,16},{12,20},{16,8},{20,12},{24,0},{28,4},{1,25},{... | collective-permute-start | bytes 393224 | tf_op jit(solution)/shard_map/ppermute | solution.py:38
  61.2 27.3 %copy-start = (bf16[128,2048]{1,0:T(8,128)(2,1)S(1)}, bf16[128,2048]{1,0:T(8,128)(2,1)}, u32[]{:S(2)}) copy-start(bf16[128,2048]{1,0:T(8,128)(2,1)} %key_ref.3) | copy-start | bytes 1572868
  61.2 27.3 %copy-start.1 = (bf16[128,2048]{1,0:T(8,128)(2,1)S(1)}, bf16[128,2048]{1,0:T(8,128)(2,1)}, u32[]{:S(2)}) copy-start(bf16[128,2048]{1,0:T(8,128)(2,1)} %value_ref.3) | copy-start | bytes 1572868
  61.3 27.3 %copy-start.3 = (bf16[128,2048]{1,0:T(8,128)(2,1)S(1)}, bf16[128,2048]{1,0:T(8,128)(2,1)}, u32[]{:S(2)}) copy-start(bf16[128,2048]{1,0:T(8,128)(2,1)} %query_ref.5) | copy-start | bytes 1572868
  61.3 27.3 %copy-start.4 = (f32[128,16]{0,1:T(8,128)S(1)}, f32[128,16]{0,1:T(8,128)}, u32[]{:S(2)}) copy-start(f32[128,16]{0,1:T(8,128)} %param.16) | copy-start | bytes 24580
  61.3 27.3 %copy-start.5 = (f32[2048]{0:T(1024)S(1)}, f32[2048]{0:T(1024)}, u32[]{:S(2)}) copy-start(f32[2048]{0:T(1024)} %param.17) | copy-start | bytes 24580
  61.3 31.0 %copy-start.6 = (s32[6,2]{0,1:T(2,128)S(1)}, s32[6,2]{0,1:T(2,128)}, u32[]{:S(2)}) copy-start(s32[6,2]{0,1:T(2,128)} %param.19) | copy-start | bytes 148
  61.3 31.0 %copy-start.7 = (f32[6,2]{0,1:T(2,128)S(1)}, f32[6,2]{0,1:T(2,128)}, u32[]{:S(2)}) copy-start(f32[6,2]{0,1:T(2,128)} %param.20) | copy-start | bytes 148
  63.9 8.2 %collective-permute-start.18 = (bf16[1024,256]{1,0:T(8,128)(2,1)S(1)}, bf16[1024,256]{1,0:T(8,128)(2,1)S(1)}, u32[]{:S(2)}, u32[]{:S(2)}) collective-permute-start(bf16[1024,256]{1,0:T(8,128)(2,1)S(1)} %constant_dynamic-update-slice_fusion.7.refs_0_), channel_id=1, source_target_pairs={{0,4},{4,0},{8,12},{12,8},{16,20},{20,16},{24,28},{28,24},{1,5},{5... | collective-permute-start | bytes 1572872 | tf_op jit(solution)/shard_map/ppermute | solution.py:38
  63.9 17.6 %collective-permute-start.23 = (bf16[8,136,128]{2,1,0:T(8,128)(2,1)S(1)}, bf16[8,136,128]{2,1,0:T(8,128)(2,1)S(1)}, u32[]{:S(2)}, u32[]{:S(2)}) collective-permute-start(bf16[8,136,128]{2,1,0:T(8,128)(2,1)S(1)} %get-tuple-element.109), channel_id=1, source_target_pairs={{0,16},{4,20},{8,24},{12,28},{16,0},{20,4},{24,8},{28,12},{1,17},{... | collective-permute-start | bytes 835592 | tf_op jit(solution)/shard_map/ppermute | solution.py:38
  65.5 9.7 %collective-permute-start.12 = (bf16[32,3072]{1,0:T(8,128)(2,1)S(1)}, bf16[32,3072]{1,0:T(8,128)(2,1)S(1)}, u32[]{:S(2)}, u32[]{:S(2)}) collective-permute-start(bf16[32,3072]{1,0:T(8,128)(2,1)S(1)} %get-tuple-element.116), channel_id=1, source_target_pairs={{0,8},{4,12},{8,0},{12,4},{16,24},{20,28},{24,16},{28,20},{1,9},{5... | collective-permute-start | bytes 589832 | tf_op jit(solution)/shard_map/ppermute | solution.py:38
  66.1 15.4 %collective-permute-start.13 = (bf16[32,3072]{1,0:T(8,128)(2,1)S(1)}, bf16[32,3072]{1,0:T(8,128)(2,1)S(1)}, u32[]{:S(2)}, u32[]{:S(2)}) collective-permute-start(bf16[32,3072]{1,0:T(8,128)(2,1)S(1)} %get-tuple-element.117), channel_id=1, source_target_pairs={{0,16},{4,20},{8,24},{12,28},{16,0},{20,4},{24,8},{28,12},{1,17},{... | collective-permute-start | bytes 589832 | tf_op jit(solution)/shard_map/ppermute | solution.py:38
  67.3 14.2 %collective-permute-start.14 = (bf16[32,3072]{1,0:T(8,128)(2,1)S(1)}, bf16[32,3072]{1,0:T(8,128)(2,1)S(1)}, u32[]{:S(2)}, u32[]{:S(2)}) collective-permute-start(bf16[32,3072]{1,0:T(8,128)(2,1)S(1)} %get-tuple-element.118), channel_id=1, source_target_pairs={{0,24},{4,28},{8,16},{12,20},{16,8},{20,12},{24,0},{28,4},{1,25},{... | collective-permute-start | bytes 589832 | tf_op jit(solution)/shard_map/ppermute | solution.py:38
  82.3 6.2 %collective-permute-start.24 = (bf16[8,128,128]{2,1,0:T(8,128)(2,1)S(1)}, bf16[8,128,128]{2,1,0:T(8,128)(2,1)S(1)}, u32[]{:S(2)}, u32[]{:S(2)}) collective-permute-start(bf16[8,128,128]{2,1,0:T(8,128)(2,1)S(1)} %get-tuple-element.140), channel_id=1, source_target_pairs={{0,4},{4,0},{8,12},{12,8},{16,20},{20,16},{24,28},{28,24},{1,5},{5... | collective-permute-start | bytes 786440 | tf_op jit(solution)/shard_map/ppermute | solution.py:38
  82.4 1.7 %collective-permute-start.19 = (bf16[16,3072]{1,0:T(8,128)(2,1)S(1)}, bf16[16,3072]{1,0:T(8,128)(2,1)S(1)}, u32[]{:S(2)}, u32[]{:S(2)}) collective-permute-start(bf16[16,3072]{1,0:T(8,128)(2,1)S(1)} %get-tuple-element.130), channel_id=1, source_target_pairs={{0,4},{4,0},{8,12},{12,8},{16,20},{20,16},{24,28},{28,24},{1,5},{5... | collective-permute-start | bytes 294920 | tf_op jit(solution)/shard_map/ppermute | solution.py:38
  84.0 8.1 %collective-permute-start.20 = (bf16[4,6144]{1,0:T(4,128)(2,1)S(1)}, bf16[4,6144]{1,0:T(4,128)(2,1)S(1)}, u32[]{:S(2)}, u32[]{:S(2)}) collective-permute-start(bf16[4,6144]{1,0:T(4,128)(2,1)S(1)} %get-tuple-element.132), channel_id=1, source_target_pairs={{0,1},{1,0},{2,3},{3,2},{4,5},{5,4},{6,7},{7,6},{8,9},{9,8},{10,11... | collective-permute-start | bytes 147464 | tf_op jit(solution)/shard_map/ppermute | solution.py:38
  84.1 8.1 %collective-permute-start.21 = (bf16[4,6144]{1,0:T(4,128)(2,1)S(1)}, bf16[4,6144]{1,0:T(4,128)(2,1)S(1)}, u32[]{:S(2)}, u32[]{:S(2)}) collective-permute-start(bf16[4,6144]{1,0:T(4,128)(2,1)S(1)} %get-tuple-element.133), channel_id=1, source_target_pairs={{0,2},{1,3},{2,0},{3,1},{4,6},{5,7},{6,4},{7,5},{8,10},{9,11},{10,... | collective-permute-start | bytes 147464 | tf_op jit(solution)/shard_map/ppermute | solution.py:38
  86.3 6.0 %collective-permute-start.22 = (bf16[4,6144]{1,0:T(4,128)(2,1)S(1)}, bf16[4,6144]{1,0:T(4,128)(2,1)S(1)}, u32[]{:S(2)}, u32[]{:S(2)}) collective-permute-start(bf16[4,6144]{1,0:T(4,128)(2,1)S(1)} %get-tuple-element.134), channel_id=1, source_target_pairs={{0,3},{1,2},{2,1},{3,0},{4,7},{5,6},{6,5},{7,4},{8,11},{9,10},{10,... | collective-permute-start | bytes 147464 | tf_op jit(solution)/shard_map/ppermute | solution.py:38
  (1 other events, 11.6 us)

commit v2 on v1

--- a/solution.py
+++ b/solution.py
@@ -149,9 +149,9 @@
 PIECES = 2
 
 
-def copies(source, target, sems):
+def copies(source, target, sems, most=PIECES):
     rows = target.shape[0]
-    pieces = max(p for p in range(1, PIECES + 1) if rows % (8 * p) == 0)
+    pieces = max(p for p in range(1, most + 1) if rows % (8 * p) == 0)
     each = rows // pieces
     return [
         pltpu.make_async_copy(
@@ -460,7 +460,7 @@
 
     def kernel(flags_ref, gate_ref, out_ref, sems):
         at = pl.ds(pl.multiple_of(flags_ref[1] * part, part), part)
-        under_way = copies(gate_ref.at[0, at], out_ref, sems)
+        under_way = copies(gate_ref.at[0, at], out_ref, sems, 6)
         for copy in under_way:
             copy.start()
         for copy in under_way:
@@ -471,7 +471,7 @@
         in_specs=[smem_spec, hbm_spec],
         out_specs=vmem_spec,
         out_shape=pltpu.VMEM((part, hidden), BF16),
-        scratch_shapes=[pltpu.SemaphoreType.DMA((PIECES,))],
+        scratch_shapes=[pltpu.SemaphoreType.DMA((6,))],
         compiler_params=params(2),
         cost_estimate=cost(0, 2 * part * hidden),
     )(flags, *in_hbm(gate_weight))
@@ -562,93 +562,40 @@
 def join_pair(flags, mine, factor, got):
     half, size, _ = mine.shape
 
-    def kernel(flags_ref, mine_ref, factor_ref, got_ref, sum_ref, sum_factor_ref, send_ref):
+    def kernel(flags_ref, mine_ref, factor_ref, got_ref, send_ref):
         odd = flags_ref[1] == 1
         for j in range(half):
             own, own_factor = mine_ref[j], factor_ref[j : j + 1]
             other, other_factor = get_message(got_ref, j)
             total = jnp.where(odd, own + own_factor * other, other + other_factor * own)
-            both = own_factor * other_factor
-            sum_ref[j] = total
-            sum_factor_ref[j : j + 1] = both
-            put_message(send_ref, j, total, both)
+            put_message(send_ref, j, total, own_factor * other_factor)
 
     return pl.pallas_call(
         kernel,
         in_specs=[smem_spec] + [vmem_spec] * 3,
-        out_specs=[vmem_spec] * 3,
-        out_shape=[
-            shape((half, size, size), F32),
-            shape((half, size), F32),
-            shape((half, size + EXTRA, size), BF16),
-        ],
-        compiler_params=params(8),
+        out_specs=vmem_spec,
+        out_shape=shape((half, size + EXTRA, size), BF16),
+        compiler_params=params(4),
     )(flags, mine, factor, got)
 
 
-def join_group(flags, bit, total, factor, before, before_factor, got):
-    half, size, _ = total.shape
-    first = before is None
-    earlier = () if first else (before, before_factor)
-
-    def kernel(flags_ref, total_ref, factor_ref, got_ref, *refs):
-        if first:
-            sum_ref, sum_factor_ref, send_ref, before_out, before_factor_out = refs
-        else:
-            (before_ref, before_factor_ref,
-             sum_ref, sum_factor_ref, send_ref, before_out, before_factor_out) = refs
-        high = ((flags_ref[0] >> bit) & 1) == 1
-        for j in range(half):
-            own, own_factor = total_ref[j], factor_ref[j : j + 1]
-            other, other_factor = get_message(got_ref, j)
-            if first:
-                prior, prior_factor = jnp.zeros_like(own), jnp.ones_like(own_factor)
-            else:
-                prior, prior_factor = before_ref[j], before_factor_ref[j : j + 1]
-            before_out[j] = jnp.where(high, prior + prior_factor * other, prior)
-            before_factor_out[j : j + 1] = jnp.where(
-                high, prior_factor * other_factor, prior_factor
-            )
-            joined = jnp.where(high, own + own_factor * other, other + other_factor * own)
-            both = own_factor * other_factor
-            sum_ref[j] = joined
-            sum_factor_ref[j : j + 1] = both
-            put_message(send_ref, j, joined, both)
-
-    return pl.pallas_call(
-        kernel,
-        in_specs=[smem_spec] + [vmem_spec] * (3 + len(earlier)),
-        out_specs=[vmem_spec] * 5,
-        out_shape=[
-            shape((half, size, size), F32),
-            shape((half, size), F32),
-            shape((half, size + EXTRA, size), BF16),
-            shape((half, size, size), F32),
-            shape((half, size), F32),
-        ],
-        compiler_params=params(12),
-    )(flags, total, factor, got, *earlier)
-
-
-def join_end(flags, bit, before, before_factor, got, mine, factor, neighbour):
+def join_end(flags, got, mine, factor, neighbour):
     half, size, _ = mine.shape
-    given = [one for one in (before, before_factor, got) if one is not None]
+    pairs = len(got) + 1
 
     def kernel(flags_ref, *refs):
-        refs = list(refs)
-        before_ref = refs.pop(0) if before is not None else None
-        before_factor_ref = refs.pop(0) if before is not None else None
-        got_ref = refs.pop(0) if got is not None else None
-        mine_ref, factor_ref, neighbour_ref, keep_ref, send_ref = refs
-        high, odd = ((flags_ref[0] >> bit) & 1) == 1, flags_ref[1] == 1
+        got_refs, refs = refs[: len(got)], refs[len(got) :]
+        mine_ref, factor_ref, neighbour_ref, keep_ref, send_ref, held = refs
+        odd = flags_ref[1] == 1
+        pair = flags_ref[0] >> 1
+        for k, one in enumerate(got_refs, 1):
+            held[pair ^ k] = one[...]
+        held[pair] = jnp.zeros(held.shape[1:], BF16)
         for j in range(half):
             state = jnp.zeros((size, size), F32)
-            if before_ref is not None:
-                state = before_ref[j]
-            if got_ref is not None:
-                other, _ = get_message(got_ref, j)
-                scaled = other if before_ref is None else before_factor_ref[j : j + 1] * other
-                state = jnp.where(high, state + scaled, state)
+            for k in range(pairs - 1):
+                other, other_factor = get_message(held.at[k], j)
+                state = jnp.where(k < pair, other + other_factor * state, state)
             other, other_factor = get_message(neighbour_ref, j)
             even_state = jnp.where(odd, other, mine_ref[j])
             even_factor = jnp.where(odd, other_factor, factor_ref[j : j + 1])
@@ -658,11 +605,12 @@
 
     return pl.pallas_call(
         kernel,
-        in_specs=[smem_spec] + [vmem_spec] * (len(given) + 3),
+        in_specs=[smem_spec] + [vmem_spec] * (len(got) + 3),
         out_specs=[vmem_spec] * 2,
         out_shape=[shape((half, size, size), BF16)] * 2,
-        compiler_params=params(8),
-    )(flags, *given, mine, factor, neighbour)
+        scratch_shapes=[pltpu.VMEM((pairs, half, size + EXTRA, size), BF16)],
+        compiler_params=params(12),
+    )(flags, *got, mine, factor, neighbour)
 
 
 def lightning(flags, lin_query, lin_key, lin_value, log_decay, lin_gain, near, far):
@@ -791,7 +739,6 @@
     count, planes = lax.axis_size("ctx"), lax.axis_size("exp")
     me = lax.axis_index("ctx").astype(jnp.int32)
     flags = jnp.stack([me, me & 1, lax.axis_index("exp").astype(jnp.int32)])
-    high = list(range(1, count.bit_length() - 1))
     chips = range(2, count, 2)
     experts = gate_weight.shape[0] * planes
     groups, size = soft_kv.shape[1], soft_kv.shape[3]
@@ -817,29 +764,19 @@
     own, other = arrange(arrived)
     rows = jnp.concatenate([own, swap(other, "ctx", 1)])
     got = [swap(rows, "ctx", j) for j in chips]
-    mine, factor, message, other_gate, *own_rest = local_states(
-        after(rows), lin_key, lin_value, log_decay, gate_weight
-    )
+    mine, factor, message, other_gate, *own_rest = local_states(after(rows), lin_key, lin_value, log_decay, gate_weight)
     *got, message = tie(*got, message)
     near = jnp.concatenate([rows, *got])
     far = swap(near, "ctx", 1)
     neighbour = swap(message, "ctx", 1)
 
     sums = gate_and_up(flags, 0, near, [gate_first, *own_rest], up_weight)
-    total, total_factor, message = join_pair(after(sums[0]), mine, factor, neighbour)
+    message = join_pair(after(sums[0]), mine, factor, neighbour)
     far, message = tie(far, message)
-    before = before_factor = got = None
-    if high:
-        got = swap(message, "ctx", 2)
+    got_states = [swap(message, "ctx", j) for j in chips]
     inner, early = gate_and_up(
         flags, 1, far, [other_gate], up_weight, sums, down_weight
     )
-    for i, b in enumerate(high[:-1]):
-        total, total_factor, message, before, before_factor = join_group(
-            after(inner), b, total, total_factor, before, before_factor, got
-        )
-        got = swap(message, "ctx", 1 << high[i + 1])
-    inner, message = tie(inner, message)
     send, early = down(flags, 1, inner, early, down_weight)
     summed = swap(send, "ctx", 1)
     keep, = down(after(send), 0, inner, early, down_weight)
@@ -860,10 +797,7 @@
     *got_sums, soft_out = tie(*got_sums, soft_out)
     own, send = fold_all(keep, got_sums)
     other = swap(send, "ctx", 1)
-    last = high[-1] if high else 0
-    state_near, state_send = join_end(
-        after(send), last, before, before_factor, got, mine, factor, neighbour
-    )
+    state_near, state_send = join_end(after(send), got_states, mine, factor, neighbour)
     state_far = swap(state_send, "ctx", 1)
     result = finish(own, other, planes)
     returned = [result[0]] + [swap(result[p], "exp", p) for p in range(1, planes)]

time: 94.2 us -> 98.7 us (1.048)
  waiting for transfers between devices: 13.5 us -> 18.4 us
  Pallas kernels: 52.9 us -> 51.7 us
    ppermute x25 -> x26, waiting for transfers between devices: 13.5 us -> 18.4 us  [swap(): lax.ppermute(value, axis, [(i, i ^ offset) for i in range(lax.axis_size(a...]
    pallas_call x2 -> x1, Pallas kernels: 2.2 us -> 0.98 us  [join_end(): pl.pallas_call(kernel, in_specs=[smem_spec] + [vmem_spec] * (len(got) + 3...]
    ppermute x25 -> x26, starting transfers between devices: 25.3 us -> 26.2 us  [swap(): lax.ppermute(value, axis, [(i, i ^ offset) for i in range(lax.axis_size(a...]
  transfers between devices with their start and end apart: 25 -> 26, of which waited for: 7 -> 7; matrix products, arithmetic and copies ran while one was open for 0% -> 0% of each run, Pallas kernels for 45% -> 35%
where the time goes in v2:
time: 98.7 us; the launch traced here: 98.5 us
  Pallas kernels  51.7 us (52%)
  starting transfers between devices  26.2 us (27%)
  waiting for transfers between devices  18.4 us (19%)
  local copies, waits for them, and re-layouts  1.13 us (1%)
  between operations  1.02 us (1%)
    ppermute x26, starting transfers between devices, swap(): lax.ppermute(value, axis, [(i, i ^ offset) for i in range(lax.axis_size(a...  26.2 us
    ppermute x26, waiting for transfers between devices, swap(): lax.ppermute(value, axis, [(i, i ^ offset) for i in range(lax.axis_size(a...  18.4 us
    pallas_call x2, Pallas kernels, gate_and_up(): pl.pallas_call(kernel, in_specs=[smem_spec, vmem_spec] + [vmem_spec] * le...  14.9 us
    pallas_call x2, Pallas kernels, down(): pl.pallas_call(kernel, in_specs=[smem_spec, vmem_spec, vmem_spec, hbm_spe...  9.67 us
    pallas_call x1, Pallas kernels, local_states(): pl.pallas_call(kernel, grid_spec=pltpu.PrefetchScalarGridSpec(num_scalar_...  8.84 us
    pallas_call x2, Pallas kernels, softmax_layer(): pl.pallas_call(kernel, grid_spec=pltpu.PrefetchScalarGridSpec(num_scalar_...  6.19 us
    pallas_call x1, Pallas kernels, fetch_gate(): pl.pallas_call(kernel, in_specs=[smem_spec, hbm_spec], out_specs=vmem_spe...  3.64 us
    pallas_call x1, Pallas kernels, lightning(): pl.pallas_call(kernel, grid_spec=pltpu.PrefetchScalarGridSpec(num_scalar_...  3.62 us
  transfers between devices with their start and end apart: 26, of which 7 were waited for; matrix products, arithmetic and copies ran while one was open for 0% of the time, Pallas kernels for 35%

profile of v2, /device:TPU:0, one launch (start us, length us, event | category | flops | bytes accessed | tf_op | source)
XLA Modules:
  0.0 98.5 jit_solution(11227863128368851072)
XLA Ops:
  0.7 1.2 %shard_map.148 = (bf16[4,6144]{1,0:T(4,128)(2,1)S(1)}, bf16[4,6144]{1,0:T(4,128)(2,1)S(1)}, bf16[4,6144]{1,0:T(4,128)(2,1)S(1)}, bf16[4,6144]{1,0:T(4,128)(2,1)S(1)}) custom-call(s32[3]{0:T(128)S(1)} %pad_add_fusion.flags_ref, s32[2,6]{1,0:T(2,128)} %bitcast.10, bf16[6,6144]{1,0:T(8,128)(2,1)} %x_ref.1), custom_call_target="tpu_custom_call" | custom-call | tf_op jit(solution)/shard_map/pallas_call | solution.py:81
  1.9 1.0 reshape.12
  3.5 2.6 %collective-permute-start = (bf16[4,6144]{1,0:T(4,128)(2,1)S(1)}, bf16[4,6144]{1,0:T(4,128)(2,1)S(1)}, u32[]{:S(2)}, u32[]{:S(2)}) collective-permute-start(bf16[4,6144]{1,0:T(4,128)(2,1)S(1)} %get-tuple-element.68), channel_id=1, source_target_pairs={{0,1},{1,0},{2,3},{3,2},{4,5},{5,4},{6,7},{7,6},{8,9},{9,8},{10,11... | collective-permute-start | bytes 147464 | tf_op jit(solution)/shard_map/ppermute | solution.py:38
  6.1 2.6 %collective-permute-start.1 = (bf16[4,6144]{1,0:T(4,128)(2,1)S(1)}, bf16[4,6144]{1,0:T(4,128)(2,1)S(1)}, u32[]{:S(2)}, u32[]{:S(2)}) collective-permute-start(bf16[4,6144]{1,0:T(4,128)(2,1)S(1)} %get-tuple-element.69), channel_id=1, source_target_pairs={{0,2},{1,3},{2,0},{3,1},{4,6},{5,7},{6,4},{7,5},{8,10},{9,11},{10,... | collective-permute-start | bytes 147464 | tf_op jit(solution)/shard_map/ppermute | solution.py:38
  8.7 3.6 %shard_map.149.refs_0_ = bf16[3072,1152]{1,0:T(8,128)(2,1)S(1)} custom-call(s32[3]{0:T(128)S(1)} %pad_add_fusion.flags_ref, bf16[2,6144,1152]{2,1,0:T(8,128)(2,1)} %gate_ref.3), custom_call_target="tpu_custom_call" | custom-call | bytes 7077888 | tf_op jit(solution)/shard_map/pallas_call | solution.py:469
  12.4 2.2 %collective-permute-done.2.refs_3_ = bf16[4,6144]{1,0:T(4,128)(2,1)S(1)} collective-permute-done((bf16[4,6144]{1,0:T(4,128)(2,1)S(1)}, bf16[4,6144]{1,0:T(4,128)(2,1)S(1)}, u32[]{:S(2)}, u32[]{:S(2)}) %collective-permute-start.2) | collective-permute-done | bytes 49184 | tf_op jit(solution)/shard_map/ppermute | solution.py:38
  14.7 1.3 %collective-permute-done.4 = bf16[16,3072]{1,0:T(8,128)(2,1)S(1)} collective-permute-done((bf16[16,3072]{1,0:T(8,128)(2,1)S(1)}, bf16[16,3072]{1,0:T(8,128)(2,1)S(1)}, u32[]{:S(2)}, u32[]{:S(2)}) %collective-permute-start.4) | collective-permute-done | bytes 98336 | tf_op jit(solution)/shard_map/ppermute | solution.py:38
  16.0 1.6 %collective-permute-start.5 = (bf16[32,3072]{1,0:T(8,128)(2,1)S(1)}, bf16[32,3072]{1,0:T(8,128)(2,1)S(1)}, u32[]{:S(2)}, u32[]{:S(2)}) collective-permute-start(bf16[32,3072]{1,0:T(8,128)(2,1)S(1)} %get-tuple-element.133), channel_id=1, source_target_pairs={{0,8},{4,12},{8,0},{12,4},{16,24},{20,28},{24,16},{28,20},{1,9},{5... | collective-permute-start | bytes 589832 | tf_op jit(solution)/shard_map/ppermute | solution.py:38
  17.6 1.5 %collective-permute-start.6 = (bf16[32,3072]{1,0:T(8,128)(2,1)S(1)}, bf16[32,3072]{1,0:T(8,128)(2,1)S(1)}, u32[]{:S(2)}, u32[]{:S(2)}) collective-permute-start(bf16[32,3072]{1,0:T(8,128)(2,1)S(1)} %get-tuple-element.133), channel_id=1, source_target_pairs={{0,16},{4,20},{8,24},{12,28},{16,0},{20,4},{24,8},{28,12},{1,17},{... | collective-permute-start | bytes 589832 | tf_op jit(solution)/shard_map/ppermute | solution.py:38
  19.6 8.8 %shard_map.151 = (f32[8,128,128]{2,1,0:T(8,128)S(1)}, f32[8,128]{1,0:T(8,128)S(1)}, bf16[8,136,128]{2,1,0:T(8,128)(2,1)S(1)}, bf16[2,3072,1152]{2,1,0:T(8,128)(2,1)S(1)}, bf16[1,3072,1152]{2,1,0:T(8,128)(2,1)S(1)}) custom-call(s32[3]{0:T(128)S(1)} %pad_add_fusion.flags_ref, bf16[128,2048]{1,0:T(8,128)(2,1)} %key_ref.3, bf16[128,2048]{1,0:T(8,128)(2,1)} %value_ref.3, ...), custom_call_target="tpu_custom_call" | custom-call | flops 134217728 | bytes 29360128 | tf_op jit(solution)/shard_map/pallas_call | solution.py:534
  29.1 7.9 %shard_map.152 = (f32[2,128,1152]{2,1,0:T(8,128)S(1)}, f32[2,128,1152]{2,1,0:T(8,128)S(1)}, bf16[3072,1152]{1,0:T(8,128)(2,1)S(1)}) custom-call(s32[3]{0:T(128)S(1)} %pad_add_fusion.flags_ref, bf16[128,3072]{1,0:T(8,128)(2,1)S(1)} %constant_dynamic-update-slice_fusion.2.x_ref, bf16[3072,1152]{1,0:T(8,128)(2,1)S(1)} %shard_map.149.refs_0_, ...), custom_call_target="tpu_custom_call" | custom-call | flops 3623878656 | bytes 28311552 | tf_op jit(solution)/shard_map/pallas_call | solution.py:260
  37.7 7.0 %shard_map.154 = (bf16[2,128,1152]{2,1,0:T(8,128)(2,1)S(1)}, bf16[2,1152,2048]{2,1,0:T(8,128)(2,1)S(1)}) custom-call(s32[3]{0:T(128)S(1)} %pad_add_fusion.flags_ref, bf16[128,3072]{1,0:T(8,128)(2,1)S(1)} %collective-permute-done.8.x_ref, bf16[2,3072,1152]{2,1,0:T(8,128)(2,1)S(1)} %get-tuple-element.92.refs_0_, bf16[2,6144,1152]{2,1,0:T(8,128)(2,1)} %refs_1_.1, ...), custom_call_target="tpu_custom_call" | custom-call | flops 3623878656 | bytes 28311552 | tf_op jit(solution)/shard_map/pallas_call | solution.py:260
  44.7 5.9 %shard_map.155 = (bf16[128,3072]{1,0:T(8,128)(2,1)S(1)}, bf16[2,1152,2048]{2,1,0:T(8,128)(2,1)S(1)}) custom-call(s32[3]{0:T(128)S(1)} %pad_add_fusion.flags_ref, bf16[2,128,1152]{2,1,0:T(8,128)(2,1)S(1)} %get-tuple-element.95.inner_ref, bf16[2,1152,2048]{2,1,0:T(8,128)(2,1)S(1)} %get-tuple-element.96.early_ref, bf16[2,1152,6144]{2,1,0:T(8,128)(2,1)} %down_ref.3), custom_call_target="tpu_custom_call" | custom-call | flops 1811939328 | bytes 14155776 | tf_op jit(solution)/shard_map/pallas_call | solution.py:355
  50.8 1.5 %collective-permute-start.14 = (bf16[256,256]{1,0:T(8,128)(2,1)S(1)}, bf16[256,256]{1,0:T(8,128)(2,1)S(1)}, u32[]{:S(2)}, u32[]{:S(2)}) collective-permute-start(bf16[256,256]{1,0:T(8,128)(2,1)S(1)} %pad_maximum_fusion), channel_id=1, source_target_pairs={{0,8},{4,12},{8,0},{12,4},{16,24},{20,28},{24,16},{28,20},{1,9},{5... | collective-permute-start | bytes 393224 | tf_op jit(solution)/shard_map/ppermute | solution.py:38
  52.2 1.5 %collective-permute-start.15 = (bf16[256,256]{1,0:T(8,128)(2,1)S(1)}, bf16[256,256]{1,0:T(8,128)(2,1)S(1)}, u32[]{:S(2)}, u32[]{:S(2)}) collective-permute-start(bf16[256,256]{1,0:T(8,128)(2,1)S(1)} %pad_maximum_fusion), channel_id=1, source_target_pairs={{0,16},{4,20},{8,24},{12,28},{16,0},{20,4},{24,8},{28,12},{1,17},{... | collective-permute-start | bytes 393224 | tf_op jit(solution)/shard_map/ppermute | solution.py:38
  54.3 3.8 %shard_map.156.keep_ref = f32[128,3072]{1,0:T(8,128)S(1)} custom-call(s32[3]{0:T(128)S(1)} %pad_add_fusion.flags_ref, bf16[2,128,1152]{2,1,0:T(8,128)(2,1)S(1)} %get-tuple-element.95.inner_ref, bf16[2,1152,2048]{2,1,0:T(8,128)(2,1)S(1)} %get-tuple-element.99.early_ref, bf16[2,1152,6144]{2,1,0:T(8,128)(2,1)} %down_ref.3), custom_call_target="tpu_custom_call" | custom-call | flops 1811939328 | bytes 14155776 | tf_op jit(solution)/shard_map/pallas_call | solution.py:355
  58.3 2.3 %collective-permute-done.15 = bf16[256,256]{1,0:T(8,128)(2,1)S(1)} collective-permute-done((bf16[256,256]{1,0:T(8,128)(2,1)S(1)}, bf16[256,256]{1,0:T(8,128)(2,1)S(1)}, u32[]{:S(2)}, u32[]{:S(2)}) %collective-permute-start.15) | collective-permute-done | bytes 131104 | tf_op jit(solution)/shard_map/ppermute | solution.py:38
  60.8 1.3 %collective-permute-start.11 = (bf16[32,3072]{1,0:T(8,128)(2,1)S(1)}, bf16[32,3072]{1,0:T(8,128)(2,1)S(1)}, u32[]{:S(2)}, u32[]{:S(2)}) collective-permute-start(bf16[32,3072]{1,0:T(8,128)(2,1)S(1)} %get-tuple-element.101), channel_id=1, source_target_pairs={{0,8},{4,12},{8,0},{12,4},{16,24},{20,28},{24,16},{28,20},{1,9},{5... | collective-permute-start | bytes 589832 | tf_op jit(solution)/shard_map/ppermute | solution.py:38
  62.8 1.5 %collective-permute-start.23 = (bf16[8,136,128]{2,1,0:T(8,128)(2,1)S(1)}, bf16[8,136,128]{2,1,0:T(8,128)(2,1)S(1)}, u32[]{:S(2)}, u32[]{:S(2)}) collective-permute-start(bf16[8,136,128]{2,1,0:T(8,128)(2,1)S(1)} %shard_map.153), channel_id=1, source_target_pairs={{0,16},{4,20},{8,24},{12,28},{16,0},{20,4},{24,8},{28,12},{1,17},{... | collective-permute-start | bytes 835592 | tf_op jit(solution)/shard_map/ppermute | solution.py:38
  64.4 1.2 %collective-permute-start.24 = (bf16[8,136,128]{2,1,0:T(8,128)(2,1)S(1)}, bf16[8,136,128]{2,1,0:T(8,128)(2,1)S(1)}, u32[]{:S(2)}, u32[]{:S(2)}) collective-permute-start(bf16[8,136,128]{2,1,0:T(8,128)(2,1)S(1)} %shard_map.153), channel_id=1, source_target_pairs={{0,24},{4,28},{8,16},{12,20},{16,8},{20,12},{24,0},{28,4},{1,25},{... | collective-permute-start | bytes 835592 | tf_op jit(solution)/shard_map/ppermute | solution.py:38
  65.5 3.1 %collective-permute-done.11.refs_0_ = bf16[32,3072]{1,0:T(8,128)(2,1)S(1)} collective-permute-done((bf16[32,3072]{1,0:T(8,128)(2,1)S(1)}, bf16[32,3072]{1,0:T(8,128)(2,1)S(1)}, u32[]{:S(2)}, u32[]{:S(2)}) %collective-permute-start.11) | collective-permute-done | bytes 196640 | tf_op jit(solution)/shard_map/ppermute | solution.py:38
  68.6 1.5 %collective-permute-start.12 = (bf16[32,3072]{1,0:T(8,128)(2,1)S(1)}, bf16[32,3072]{1,0:T(8,128)(2,1)S(1)}, u32[]{:S(2)}, u32[]{:S(2)}) collective-permute-start(bf16[32,3072]{1,0:T(8,128)(2,1)S(1)} %get-tuple-element.102), channel_id=1, source_target_pairs={{0,16},{4,20},{8,24},{12,28},{16,0},{20,4},{24,8},{28,12},{1,17},{... | collective-permute-start | bytes 589832 | tf_op jit(solution)/shard_map/ppermute | solution.py:38
  70.1 1.2 %collective-permute-start.13 = (bf16[32,3072]{1,0:T(8,128)(2,1)S(1)}, bf16[32,3072]{1,0:T(8,128)(2,1)S(1)}, u32[]{:S(2)}, u32[]{:S(2)}) collective-permute-start(bf16[32,3072]{1,0:T(8,128)(2,1)S(1)} %get-tuple-element.103), channel_id=1, source_target_pairs={{0,24},{4,28},{8,16},{12,20},{16,8},{20,12},{24,0},{28,4},{1,25},{... | collective-permute-start | bytes 589832 | tf_op jit(solution)/shard_map/ppermute | solution.py:38
  71.3 3.1 %shard_map.158.refs_1_ = bf16[128,2048]{1,0:T(8,128)(2,1)} custom-call(s32[3]{0:T(128)S(1)} %pad_add_fusion.flags_ref, bf16[128,2048]{1,0:T(8,128)(2,1)S(1)} %copy-done.2, bf16[1024,256]{1,0:T(8,128)(2,1)S(1)} %constant_dynamic-update-slice_fusion.7.refs_0_), custom_call_target="tpu_custom_call" | custom-call | flops 536870912 | bytes 524288 | tf_op jit(solution)/shard_map/pallas_call | solution.py:710
  74.4 3.1 %shard_map.159 = bf16[128,2048]{1,0:T(8,128)(2,1)} custom-call(s32[3]{0:T(128)S(1)} %pad_add_fusion.flags_ref, bf16[128,2048]{1,0:T(8,128)(2,1)S(1)} %copy-done.2, bf16[1024,256]{1,0:T(8,128)(2,1)S(1)} %collective-permute-done.17.refs_0_, bf16[128,2048]{1,0:T(8,128)(2,1)} %shard_map.158.refs_1_), custom_call_target="tpu_custom_call", output_to_operand_aliasing={{}: (3, {})} | custom-call | flops 536870912 | bytes 524288 | tf_op jit(solution)/shard_map/pallas_call | solution.py:710
  77.5 8.2 %collective-permute-done.12.refs_1_ = bf16[32,3072]{1,0:T(8,128)(2,1)S(1)} collective-permute-done((bf16[32,3072]{1,0:T(8,128)(2,1)S(1)}, bf16[32,3072]{1,0:T(8,128)(2,1)S(1)}, u32[]{:S(2)}, u32[]{:S(2)}) %collective-permute-start.12) | collective-permute-done | bytes 196640 | tf_op jit(solution)/shard_map/ppermute | solution.py:38
  85.8 1.0 shard_map.162
  87.4 1.2 %collective-permute-done.18.other_ref = bf16[16,3072]{1,0:T(8,128)(2,1)S(1)} collective-permute-done((bf16[16,3072]{1,0:T(8,128)(2,1)S(1)}, bf16[16,3072]{1,0:T(8,128)(2,1)S(1)}, u32[]{:S(2)}, u32[]{:S(2)}) %collective-permute-start.18) | collective-permute-done | bytes 98336 | tf_op jit(solution)/shard_map/ppermute | solution.py:38
  88.6 2.2 %collective-permute-start.20 = (bf16[4,6144]{1,0:T(4,128)(2,1)S(1)}, bf16[4,6144]{1,0:T(4,128)(2,1)S(1)}, u32[]{:S(2)}, u32[]{:S(2)}) collective-permute-start(bf16[4,6144]{1,0:T(4,128)(2,1)S(1)} %get-tuple-element.118), channel_id=1, source_target_pairs={{0,2},{1,3},{2,0},{3,1},{4,6},{5,7},{6,4},{7,5},{8,10},{9,11},{10,... | collective-permute-start | bytes 147464 | tf_op jit(solution)/shard_map/ppermute | solution.py:38
  90.8 2.2 %collective-permute-start.21 = (bf16[4,6144]{1,0:T(4,128)(2,1)S(1)}, bf16[4,6144]{1,0:T(4,128)(2,1)S(1)}, u32[]{:S(2)}, u32[]{:S(2)}) collective-permute-start(bf16[4,6144]{1,0:T(4,128)(2,1)S(1)} %get-tuple-element.119), channel_id=1, source_target_pairs={{0,3},{1,2},{2,1},{3,0},{4,7},{5,6},{6,5},{7,4},{8,11},{9,10},{10,... | collective-permute-start | bytes 147464 | tf_op jit(solution)/shard_map/ppermute | solution.py:38
  93.0 3.6 %shard_map.163 = bf16[128,2048]{1,0:T(8,128)(2,1)} custom-call(s32[3]{0:T(128)S(1)} %pad_add_fusion.flags_ref, bf16[128,2048]{1,0:T(8,128)(2,1)S(1)} %copy-done.3, bf16[128,2048]{1,0:T(8,128)(2,1)S(1)} %copy-done, bf16[128,2048]{1,0:T(8,128)(2,1)S(1)} %copy-done.1, f32[16,128]{1,0:T(8,128)S(1)} %bitcast.8, f32[1,2048]{1,0:T(1,128)S(1)} %bitcast.9, ...), custom_call_target="tpu_custom_call" | custom-call | flops 201326592 | bytes 2097152 | tf_op jit(solution)/shard_map/pallas_call | solution.py:653
  96.8 1.7 %shard_map.164 = bf16[6,6144]{1,0:T(8,128)(2,1)} custom-call(s32[3]{0:T(128)S(1)} %pad_add_fusion.flags_ref, s32[2,6]{1,0:T(2,128)S(1)} %bitcast.11, f32[2,6]{1,0:T(2,128)S(1)} %bitcast.12, bf16[4,6144]{1,0:T(4,128)(2,1)S(1)} %get-tuple-element.126.refs_0_, bf16[4,6144]{1,0:T(4,128)(2,1)S(1)} %collective-permute-done.19.refs_1_, ...), custom_call_target="tpu_custom_call" | custom-call | tf_op jit(solution)/shard_map/pallas_call | solution.py:136
  (66 shorter events, 5.3 us)
Async XLA Ops:
  2.9 5.8 %collective-permute-start.3 = (bf16[128,256]{1,0:T(8,128)(2,1)S(1)}, bf16[128,256]{1,0:T(8,128)(2,1)S(1)}, u32[]{:S(2)}, u32[]{:S(2)}) collective-permute-start(bf16[128,256]{1,0:T(8,128)(2,1)S(1)} %get-tuple-element.132), channel_id=1, source_target_pairs={{0,4},{4,0},{8,12},{12,8},{16,20},{20,16},{24,28},{28,24},{1,5},{5... | collective-permute-start | bytes 196616 | tf_op jit(solution)/shard_map/ppermute | solution.py:38
  3.5 8.9 %collective-permute-start = (bf16[4,6144]{1,0:T(4,128)(2,1)S(1)}, bf16[4,6144]{1,0:T(4,128)(2,1)S(1)}, u32[]{:S(2)}, u32[]{:S(2)}) collective-permute-start(bf16[4,6144]{1,0:T(4,128)(2,1)S(1)} %get-tuple-element.68), channel_id=1, source_target_pairs={{0,1},{1,0},{2,3},{3,2},{4,5},{5,4},{6,7},{7,6},{8,9},{9,8},{10,11... | collective-permute-start | bytes 147464 | tf_op jit(solution)/shard_map/ppermute | solution.py:38
  6.1 6.3 %collective-permute-start.1 = (bf16[4,6144]{1,0:T(4,128)(2,1)S(1)}, bf16[4,6144]{1,0:T(4,128)(2,1)S(1)}, u32[]{:S(2)}, u32[]{:S(2)}) collective-permute-start(bf16[4,6144]{1,0:T(4,128)(2,1)S(1)} %get-tuple-element.69), channel_id=1, source_target_pairs={{0,2},{1,3},{2,0},{3,1},{4,6},{5,7},{6,4},{7,5},{8,10},{9,11},{10,... | collective-permute-start | bytes 147464 | tf_op jit(solution)/shard_map/ppermute | solution.py:38
  8.7 5.9 %collective-permute-start.2 = (bf16[4,6144]{1,0:T(4,128)(2,1)S(1)}, bf16[4,6144]{1,0:T(4,128)(2,1)S(1)}, u32[]{:S(2)}, u32[]{:S(2)}) collective-permute-start(bf16[4,6144]{1,0:T(4,128)(2,1)S(1)} %get-tuple-element.70), channel_id=1, source_target_pairs={{0,3},{1,2},{2,1},{3,0},{4,7},{5,6},{6,5},{7,4},{8,11},{9,10},{10,... | collective-permute-start | bytes 147464 | tf_op jit(solution)/shard_map/ppermute | solution.py:38
  14.6 1.4 %collective-permute-start.4 = (bf16[16,3072]{1,0:T(8,128)(2,1)S(1)}, bf16[16,3072]{1,0:T(8,128)(2,1)S(1)}, u32[]{:S(2)}, u32[]{:S(2)}) collective-permute-start(bf16[16,3072]{1,0:T(8,128)(2,1)S(1)} %get-tuple-element.78), channel_id=1, source_target_pairs={{0,4},{4,0},{8,12},{12,8},{16,20},{20,16},{24,28},{28,24},{1,5},{5... | collective-permute-start | bytes 294920 | tf_op jit(solution)/shard_map/ppermute | solution.py:38
  16.0 12.4 %collective-permute-start.5 = (bf16[32,3072]{1,0:T(8,128)(2,1)S(1)}, bf16[32,3072]{1,0:T(8,128)(2,1)S(1)}, u32[]{:S(2)}, u32[]{:S(2)}) collective-permute-start(bf16[32,3072]{1,0:T(8,128)(2,1)S(1)} %get-tuple-element.133), channel_id=1, source_target_pairs={{0,8},{4,12},{8,0},{12,4},{16,24},{20,28},{24,16},{28,20},{1,9},{5... | collective-permute-start | bytes 589832 | tf_op jit(solution)/shard_map/ppermute | solution.py:38
  17.6 10.9 %collective-permute-start.6 = (bf16[32,3072]{1,0:T(8,128)(2,1)S(1)}, bf16[32,3072]{1,0:T(8,128)(2,1)S(1)}, u32[]{:S(2)}, u32[]{:S(2)}) collective-permute-start(bf16[32,3072]{1,0:T(8,128)(2,1)S(1)} %get-tuple-element.133), channel_id=1, source_target_pairs={{0,16},{4,20},{8,24},{12,28},{16,0},{20,4},{24,8},{28,12},{1,17},{... | collective-permute-start | bytes 589832 | tf_op jit(solution)/shard_map/ppermute | solution.py:38
  19.1 9.4 %collective-permute-start.7 = (bf16[32,3072]{1,0:T(8,128)(2,1)S(1)}, bf16[32,3072]{1,0:T(8,128)(2,1)S(1)}, u32[]{:S(2)}, u32[]{:S(2)}) collective-permute-start(bf16[32,3072]{1,0:T(8,128)(2,1)S(1)} %get-tuple-element.133), channel_id=1, source_target_pairs={{0,24},{4,28},{8,16},{12,20},{16,8},{20,12},{24,0},{28,4},{1,25},{... | collective-permute-start | bytes 589832 | tf_op jit(solution)/shard_map/ppermute | solution.py:38
  28.5 9.2 %collective-permute-start.8 = (bf16[128,3072]{1,0:T(8,128)(2,1)S(1)}, bf16[128,3072]{1,0:T(8,128)(2,1)S(1)}, u32[]{:S(2)}, u32[]{:S(2)}) collective-permute-start(bf16[128,3072]{1,0:T(8,128)(2,1)S(1)} %constant_dynamic-update-slice_fusion.2.x_ref), channel_id=1, source_target_pairs={{0,4},{4,0},{8,12},{12,8},{16,20},{20,16},{24,28},{28,24},{1,5},{5... | collective-permute-start | bytes 2359304 | tf_op jit(solution)/shard_map/ppermute | solution.py:38
  28.6 8.4 %collective-permute-start.9 = (bf16[8,136,128]{2,1,0:T(8,128)(2,1)S(1)}, bf16[8,136,128]{2,1,0:T(8,128)(2,1)S(1)}, u32[]{:S(2)}, u32[]{:S(2)}) collective-permute-start(bf16[8,136,128]{2,1,0:T(8,128)(2,1)S(1)} %get-tuple-element.90), channel_id=1, source_target_pairs={{0,4},{4,0},{8,12},{12,8},{16,20},{20,16},{24,28},{28,24},{1,5},{5... | collective-permute-start | bytes 835592 | tf_op jit(solution)/shard_map/ppermute | solution.py:38
  50.6 7.5 %collective-permute-start.10 = (bf16[128,3072]{1,0:T(8,128)(2,1)S(1)}, bf16[128,3072]{1,0:T(8,128)(2,1)S(1)}, u32[]{:S(2)}, u32[]{:S(2)}) collective-permute-start(bf16[128,3072]{1,0:T(8,128)(2,1)S(1)} %get-tuple-element.97), channel_id=1, source_target_pairs={{0,4},{4,0},{8,12},{12,8},{16,20},{20,16},{24,28},{28,24},{1,5},{5... | collective-permute-start | bytes 2359304 | tf_op jit(solution)/shard_map/ppermute | solution.py:38
  50.8 7.5 %collective-permute-start.14 = (bf16[256,256]{1,0:T(8,128)(2,1)S(1)}, bf16[256,256]{1,0:T(8,128)(2,1)S(1)}, u32[]{:S(2)}, u32[]{:S(2)}) collective-permute-start(bf16[256,256]{1,0:T(8,128)(2,1)S(1)} %pad_maximum_fusion), channel_id=1, source_target_pairs={{0,8},{4,12},{8,0},{12,4},{16,24},{20,28},{24,16},{28,20},{1,9},{5... | collective-permute-start | bytes 393224 | tf_op jit(solution)/shard_map/ppermute | solution.py:38
  52.2 8.4 %collective-permute-start.15 = (bf16[256,256]{1,0:T(8,128)(2,1)S(1)}, bf16[256,256]{1,0:T(8,128)(2,1)S(1)}, u32[]{:S(2)}, u32[]{:S(2)}) collective-permute-start(bf16[256,256]{1,0:T(8,128)(2,1)S(1)} %pad_maximum_fusion), channel_id=1, source_target_pairs={{0,16},{4,20},{8,24},{12,28},{16,0},{20,4},{24,8},{28,12},{1,17},{... | collective-permute-start | bytes 393224 | tf_op jit(solution)/shard_map/ppermute | solution.py:38
  53.8 6.8 %collective-permute-start.16 = (bf16[256,256]{1,0:T(8,128)(2,1)S(1)}, bf16[256,256]{1,0:T(8,128)(2,1)S(1)}, u32[]{:S(2)}, u32[]{:S(2)}) collective-permute-start(bf16[256,256]{1,0:T(8,128)(2,1)S(1)} %pad_maximum_fusion), channel_id=1, source_target_pairs={{0,24},{4,28},{8,16},{12,20},{16,8},{20,12},{24,0},{28,4},{1,25},{... | collective-permute-start | bytes 393224 | tf_op jit(solution)/shard_map/ppermute | solution.py:38
  58.1 35.0 %copy-start = (bf16[128,2048]{1,0:T(8,128)(2,1)S(1)}, bf16[128,2048]{1,0:T(8,128)(2,1)}, u32[]{:S(2)}) copy-start(bf16[128,2048]{1,0:T(8,128)(2,1)} %key_ref.3) | copy-start | bytes 1572868
  58.1 35.0 %copy-start.1 = (bf16[128,2048]{1,0:T(8,128)(2,1)S(1)}, bf16[128,2048]{1,0:T(8,128)(2,1)}, u32[]{:S(2)}) copy-start(bf16[128,2048]{1,0:T(8,128)(2,1)} %value_ref.3) | copy-start | bytes 1572868
  58.1 34.9 %copy-start.3 = (bf16[128,2048]{1,0:T(8,128)(2,1)S(1)}, bf16[128,2048]{1,0:T(8,128)(2,1)}, u32[]{:S(2)}) copy-start(bf16[128,2048]{1,0:T(8,128)(2,1)} %query_ref.5) | copy-start | bytes 1572868
  58.1 34.9 %copy-start.4 = (f32[128,16]{0,1:T(8,128)S(1)}, f32[128,16]{0,1:T(8,128)}, u32[]{:S(2)}) copy-start(f32[128,16]{0,1:T(8,128)} %param.16) | copy-start | bytes 24580
  58.1 38.7 %copy-start.6 = (s32[6,2]{0,1:T(2,128)S(1)}, s32[6,2]{0,1:T(2,128)}, u32[]{:S(2)}) copy-start(s32[6,2]{0,1:T(2,128)} %param.19) | copy-start | bytes 148
  58.1 38.7 %copy-start.7 = (f32[6,2]{0,1:T(2,128)S(1)}, f32[6,2]{0,1:T(2,128)}, u32[]{:S(2)}) copy-start(f32[6,2]{0,1:T(2,128)} %param.20) | copy-start | bytes 148
  60.7 9.4 %collective-permute-start.17 = (bf16[1024,256]{1,0:T(8,128)(2,1)S(1)}, bf16[1024,256]{1,0:T(8,128)(2,1)S(1)}, u32[]{:S(2)}, u32[]{:S(2)}) collective-permute-start(bf16[1024,256]{1,0:T(8,128)(2,1)S(1)} %constant_dynamic-update-slice_fusion.7.refs_0_), channel_id=1, source_target_pairs={{0,4},{4,0},{8,12},{12,8},{16,20},{20,16},{24,28},{28,24},{1,5},{5... | collective-permute-start | bytes 1572872 | tf_op jit(solution)/shard_map/ppermute | solution.py:38
  60.8 7.8 %collective-permute-start.11 = (bf16[32,3072]{1,0:T(8,128)(2,1)S(1)}, bf16[32,3072]{1,0:T(8,128)(2,1)S(1)}, u32[]{:S(2)}, u32[]{:S(2)}) collective-permute-start(bf16[32,3072]{1,0:T(8,128)(2,1)S(1)} %get-tuple-element.101), channel_id=1, source_target_pairs={{0,8},{4,12},{8,0},{12,4},{16,24},{20,28},{24,16},{28,20},{1,9},{5... | collective-permute-start | bytes 589832 | tf_op jit(solution)/shard_map/ppermute | solution.py:38
  62.1 23.7 %collective-permute-start.22 = (bf16[8,136,128]{2,1,0:T(8,128)(2,1)S(1)}, bf16[8,136,128]{2,1,0:T(8,128)(2,1)S(1)}, u32[]{:S(2)}, u32[]{:S(2)}) collective-permute-start(bf16[8,136,128]{2,1,0:T(8,128)(2,1)S(1)} %shard_map.153), channel_id=1, source_target_pairs={{0,8},{4,12},{8,0},{12,4},{16,24},{20,28},{24,16},{28,20},{1,9},{5... | collective-permute-start | bytes 835592 | tf_op jit(solution)/shard_map/ppermute | solution.py:38
  62.8 22.9 %collective-permute-start.23 = (bf16[8,136,128]{2,1,0:T(8,128)(2,1)S(1)}, bf16[8,136,128]{2,1,0:T(8,128)(2,1)S(1)}, u32[]{:S(2)}, u32[]{:S(2)}) collective-permute-start(bf16[8,136,128]{2,1,0:T(8,128)(2,1)S(1)} %shard_map.153), channel_id=1, source_target_pairs={{0,16},{4,20},{8,24},{12,28},{16,0},{20,4},{24,8},{28,12},{1,17},{... | collective-permute-start | bytes 835592 | tf_op jit(solution)/shard_map/ppermute | solution.py:38
  64.4 21.4 %collective-permute-start.24 = (bf16[8,136,128]{2,1,0:T(8,128)(2,1)S(1)}, bf16[8,136,128]{2,1,0:T(8,128)(2,1)S(1)}, u32[]{:S(2)}, u32[]{:S(2)}) collective-permute-start(bf16[8,136,128]{2,1,0:T(8,128)(2,1)S(1)} %shard_map.153), channel_id=1, source_target_pairs={{0,24},{4,28},{8,16},{12,20},{16,8},{20,12},{24,0},{28,4},{1,25},{... | collective-permute-start | bytes 835592 | tf_op jit(solution)/shard_map/ppermute | solution.py:38
  68.6 17.1 %collective-permute-start.12 = (bf16[32,3072]{1,0:T(8,128)(2,1)S(1)}, bf16[32,3072]{1,0:T(8,128)(2,1)S(1)}, u32[]{:S(2)}, u32[]{:S(2)}) collective-permute-start(bf16[32,3072]{1,0:T(8,128)(2,1)S(1)} %get-tuple-element.102), channel_id=1, source_target_pairs={{0,16},{4,20},{8,24},{12,28},{16,0},{20,4},{24,8},{28,12},{1,17},{... | collective-permute-start | bytes 589832 | tf_op jit(solution)/shard_map/ppermute | solution.py:38
  70.1 15.6 %collective-permute-start.13 = (bf16[32,3072]{1,0:T(8,128)(2,1)S(1)}, bf16[32,3072]{1,0:T(8,128)(2,1)S(1)}, u32[]{:S(2)}, u32[]{:S(2)}) collective-permute-start(bf16[32,3072]{1,0:T(8,128)(2,1)S(1)} %get-tuple-element.103), channel_id=1, source_target_pairs={{0,24},{4,28},{8,16},{12,20},{16,8},{20,12},{24,0},{28,4},{1,25},{... | collective-permute-start | bytes 589832 | tf_op jit(solution)/shard_map/ppermute | solution.py:38
  86.8 6.2 %collective-permute-start.25 = (bf16[8,128,128]{2,1,0:T(8,128)(2,1)S(1)}, bf16[8,128,128]{2,1,0:T(8,128)(2,1)S(1)}, u32[]{:S(2)}, u32[]{:S(2)}) collective-permute-start(bf16[8,128,128]{2,1,0:T(8,128)(2,1)S(1)} %get-tuple-element.124), channel_id=1, source_target_pairs={{0,4},{4,0},{8,12},{12,8},{16,20},{20,16},{24,28},{28,24},{1,5},{5... | collective-permute-start | bytes 786440 | tf_op jit(solution)/shard_map/ppermute | solution.py:38
  86.9 1.7 %collective-permute-start.18 = (bf16[16,3072]{1,0:T(8,128)(2,1)S(1)}, bf16[16,3072]{1,0:T(8,128)(2,1)S(1)}, u32[]{:S(2)}, u32[]{:S(2)}) collective-permute-start(bf16[16,3072]{1,0:T(8,128)(2,1)S(1)} %get-tuple-element.115), channel_id=1, source_target_pairs={{0,4},{4,0},{8,12},{12,8},{16,20},{20,16},{24,28},{28,24},{1,5},{5... | collective-permute-start | bytes 294920 | tf_op jit(solution)/shard_map/ppermute | solution.py:38
  88.6 8.1 %collective-permute-start.19 = (bf16[4,6144]{1,0:T(4,128)(2,1)S(1)}, bf16[4,6144]{1,0:T(4,128)(2,1)S(1)}, u32[]{:S(2)}, u32[]{:S(2)}) collective-permute-start(bf16[4,6144]{1,0:T(4,128)(2,1)S(1)} %get-tuple-element.117), channel_id=1, source_target_pairs={{0,1},{1,0},{2,3},{3,2},{4,5},{5,4},{6,7},{7,6},{8,9},{9,8},{10,11... | collective-permute-start | bytes 147464 | tf_op jit(solution)/shard_map/ppermute | solution.py:38
  88.6 8.0 %collective-permute-start.20 = (bf16[4,6144]{1,0:T(4,128)(2,1)S(1)}, bf16[4,6144]{1,0:T(4,128)(2,1)S(1)}, u32[]{:S(2)}, u32[]{:S(2)}) collective-permute-start(bf16[4,6144]{1,0:T(4,128)(2,1)S(1)} %get-tuple-element.118), channel_id=1, source_target_pairs={{0,2},{1,3},{2,0},{3,1},{4,6},{5,7},{6,4},{7,5},{8,10},{9,11},{10,... | collective-permute-start | bytes 147464 | tf_op jit(solution)/shard_map/ppermute | solution.py:38
  90.8 6.0 %collective-permute-start.21 = (bf16[4,6144]{1,0:T(4,128)(2,1)S(1)}, bf16[4,6144]{1,0:T(4,128)(2,1)S(1)}, u32[]{:S(2)}, u32[]{:S(2)}) collective-permute-start(bf16[4,6144]{1,0:T(4,128)(2,1)S(1)} %get-tuple-element.119), channel_id=1, source_target_pairs={{0,3},{1,2},{2,1},{3,0},{4,7},{5,6},{6,5},{7,4},{8,11},{9,10},{10,... | collective-permute-start | bytes 147464 | tf_op jit(solution)/shard_map/ppermute | solution.py:38
  (2 other events, 52.0 us)
